TPU v7x, 512 devices: a whole 4x8x8 slice. The times are simulated.
512 devices in a mesh: cp: 64 (over x, y, core), dp: 8 (over z).
Axes of the slice: x: 4, y: 8, z: 8, core: 2. Of those that a mesh axis runs over, the one named last changes fastest.
Arguments:
- queries: bfloat16 [65536, 4096], P(('dp', 'cp')), parts along dimension 0, may hold values from -200 to 200
- keys: bfloat16 [65536, 512], P(('dp', 'cp')), parts along dimension 0, may hold values from -6 to 6
- values: bfloat16 [65536, 512], P(('dp', 'cp')), parts along dimension 0, may hold values from -6 to 6
- segments: int32 [65536], P('dp'), parts along dimension 0, may hold values from 0 to 15, never falling along the last dimension, each value on 1 to 1024 neighbouring positions
- loss_mask: int32 [65536], P(('dp', 'cp')), parts along dimension 0, may hold values 0 or 1
- grad_out: bfloat16 [65536, 4096], P(('dp', 'cp')), parts along dimension 0, may hold values from -6 to 6
Outputs:
- grad_q: bfloat16 [65536, 4096], P(('dp', 'cp')), parts along dimension 0
- grad_k: bfloat16 [65536, 512], P(('dp', 'cp')), parts along dimension 0
- grad_v: bfloat16 [65536, 512], P(('dp', 'cp')), parts along dimension 0
There are 8 independent parts, one for each index of `dp`. A program takes and returns all parts, laid end to end along the dimension named above; each array names one. Nothing has to cross between parts.
Inputs may be any that keep to these rules, and one draw needn't show every extreme that they name: `segments`: document ids never fall along the sequence; every document holds 1 to 1024 tokens and one holds exactly 1024.
All inputs are finite; a program needn't handle non-finite values. No bound on the sum of `loss_mask` on one device may be relied on, other than what follows from the above.
Results may differ from a plain program's by a relative error of at most 0.019.
Values may be sent and summed in bfloat16 or wider, within the bound.
A program may use at most 64 MiB of HBM per device.

v0:
```python
import jax
import jax.numpy as jnp
from jax import lax
from jax.sharding import PartitionSpec as P

HD = 128
RADIUS = 8


def passed_along(x, axis, by):
    devices = lax.axis_size(axis)
    pairs = [(i, i + by) for i in range(devices) if 0 <= i + by < devices]
    return lax.ppermute(x, axis, pairs)


def per_device(queries, keys, values, segments, loss_mask, grad_out):
    rows = queries.shape[0]
    kv_width = keys.shape[1]
    head_dim = HD
    kv_heads = kv_width // head_dim
    group = queries.shape[1] // kv_width
    span = RADIUS + 1
    here = lax.axis_index("cp")
    scale = head_dim ** (-0.5)
    stacked = jnp.stack([keys, values])
    sections = []
    reach = 1
    for level in range(8):
        if reach < span:
            sections.append((reach, min(reach, span - reach)))
            reach = reach * 2

    def forward_step(carry, unused):
        moved = passed_along(carry, "cp", 1)
        return (moved, moved)

    last, later = lax.scan(forward_step, stacked, None, length=RADIUS)
    held = jnp.concatenate([stacked[None], later], 0)
    ordered = held[::-1]
    key_win = ordered[:, 0].reshape(span * rows, kv_width)
    val_win = ordered[:, 1].reshape(span * rows, kv_width)
    seg_pad = jnp.concatenate([jnp.full((RADIUS * rows,), -1, jnp.int32), segments], 0)
    key_seg = lax.dynamic_slice_in_dim(seg_pad, here * rows, span * rows, 0)
    query_seg = lax.dynamic_slice_in_dim(segments, here * rows, rows, 0)
    query_pos = here * rows + jnp.arange(rows, dtype=jnp.int32)
    key_pos = (here - RADIUS) * rows + jnp.arange(span * rows, dtype=jnp.int32)
    allowed = (query_seg[:, None] == key_seg[None, :]) & (key_pos[None, :] <= query_pos[:, None])
    masked = grad_out * loss_mask[:, None].astype(jnp.bfloat16)

    def per_group(index, carry):
        grad_query, grad_keys, grad_vals = carry
        column = index * group * head_dim
        q_block = lax.dynamic_slice_in_dim(queries, column, group * head_dim, 1).reshape(
            rows, group, head_dim
        )
        o_block = lax.dynamic_slice_in_dim(masked, column, group * head_dim, 1).reshape(
            rows, group, head_dim
        )
        k_block = lax.dynamic_slice_in_dim(key_win, index * head_dim, head_dim, 1)
        v_block = lax.dynamic_slice_in_dim(val_win, index * head_dim, head_dim, 1)
        scores = (
            jnp.einsum("tgd,kd->gtk", q_block, k_block, preferred_element_type=jnp.float32) * scale
        )
        scores = jnp.where(allowed[None], scores, -1e30)
        peak = jnp.max(scores, axis=-1, keepdims=True)
        expo = jnp.exp(scores - peak)
        probs = expo / jnp.sum(expo, axis=-1, keepdims=True)
        probs_b = probs.astype(jnp.bfloat16)
        attended = jnp.einsum(
            "gtk,kd->tgd", probs_b, v_block, preferred_element_type=jnp.float32
        ).astype(jnp.bfloat16)
        delta = jnp.sum(o_block.astype(jnp.float32) * attended.astype(jnp.float32), axis=-1)
        dprobs = jnp.einsum("tgd,kd->gtk", o_block, v_block, preferred_element_type=jnp.float32)
        dscores = (probs * (dprobs - jnp.transpose(delta)[:, :, None])).astype(jnp.bfloat16)
        dq = jnp.einsum("gtk,kd->tgd", dscores, k_block, preferred_element_type=jnp.float32) * scale
        dk = jnp.einsum("gtk,tgd->kd", dscores, q_block, preferred_element_type=jnp.float32) * scale
        dv = jnp.einsum("gtk,tgd->kd", probs_b, o_block, preferred_element_type=jnp.float32)
        grad_query = lax.dynamic_update_slice_in_dim(
            grad_query, dq.reshape(rows, group * head_dim), column, 1
        )
        grad_keys = lax.dynamic_update_slice_in_dim(grad_keys, dk, index * head_dim, 1)
        grad_vals = lax.dynamic_update_slice_in_dim(grad_vals, dv, index * head_dim, 1)
        return (grad_query, grad_keys, grad_vals)

    start_state = (
        jnp.zeros(queries.shape, jnp.float32),
        jnp.zeros((span * rows, kv_width), jnp.float32),
        jnp.zeros((span * rows, kv_width), jnp.float32),
    )
    grad_query, grad_keys, grad_vals = lax.fori_loop(0, kv_heads, per_group, start_state)
    partials = jnp.stack(
        [grad_keys.reshape(span, rows, kv_width), grad_vals.reshape(span, rows, kv_width)], 1
    )
    by_offset = partials[::-1]

    def backward_step(carry, term):
        moved = passed_along(carry, "cp", -1)
        return (moved + term, None)

    total, unused = lax.scan(backward_step, by_offset[RADIUS], by_offset[:RADIUS][::-1])
    return (
        grad_query.astype(jnp.bfloat16),
        total[0].astype(jnp.bfloat16),
        total[1].astype(jnp.bfloat16),
    )


def solution(mesh):
    placed = (
        P(("dp", "cp"), None),
        P(("dp", "cp"), None),
        P(("dp", "cp"), None),
        P("dp"),
        P(("dp", "cp")),
        P(("dp", "cp"), None),
    )
    return jax.shard_map(
        per_device,
        mesh=mesh,
        in_specs=placed,
        out_specs=(P(("dp", "cp"), None), P(("dp", "cp"), None), P(("dp", "cp"), None)),
        check_vma=False,
    )
```

profile of v0, /device:TPU:57, one launch (start us, length us, event | category | flops | bytes accessed | tf_op | source)
XLA Modules:
  0.0 279.5 jit_solution(12759985526755012942)
XLA Ops:
  6.5 80.6 %while.42 = (s32[]{:T(128)}, bf16[2,128,512]{2,1,0:T(8,128)(2,1)S(1)}, bf16[8,2,128,512]{3,2,1,0:T(8,128)(2,1)}, s32[]{:T(128)}) while((s32[]{:T(128)}, bf16[2,128,512]{2,1,0:T(8,128)(2,1)S(1)}, bf16[8,2,128,512]{3,2,1,0:T(8,128)(2,1)}, s32[]{:T(128)}) %tuple.77), condition=%wide.region_1.2_spmd, body=%wide.region_0.1_spmd.sunk | while | flops 2 | bytes 2097257 | solution.py:37
  6.5 2.9 %collective-permute-start = (bf16[2,128,512]{2,1,0:T(8,128)(2,1)S(1)}, bf16[2,128,512]{2,1,0:T(8,128)(2,1)S(1)}, u32[]{:S(2)}, u32[]{:S(2)}) collective-permute-start(bf16[2,128,512]{2,1,0:T(8,128)(2,1)S(1)} %get-tuple-element.472), channel_id=1, source_target_pairs={{0,8},{8,16},{16,24},{24,32},{32,40},{40,48},{48,56},{56,64},{64,7... | collective-permute-start | bytes 786440 | tf_op jit(solution)/shard_map/while/body/eval_jaxpr/ppermute | solution.py:13
  9.4 3.3 %collective-permute-done = bf16[2,128,512]{2,1,0:T(8,128)(2,1)S(1)} collective-permute-done((bf16[2,128,512]{2,1,0:T(8,128)(2,1)S(1)}, bf16[2,128,512]{2,1,0:T(8,128)(2,1)S(1)}, u32[]{:S(2)}, u32[]{:S(2)}) %collective-permute-start) | collective-permute-done | bytes 262176 | tf_op jit(solution)/shard_map/while/body/eval_jaxpr/ppermute | solution.py:13
  13.4 6.5 %collective-permute-start = (bf16[2,128,512]{2,1,0:T(8,128)(2,1)S(1)}, bf16[2,128,512]{2,1,0:T(8,128)(2,1)S(1)}, u32[]{:S(2)}, u32[]{:S(2)}) collective-permute-start(bf16[2,128,512]{2,1,0:T(8,128)(2,1)S(1)} %get-tuple-element.472), channel_id=1, source_target_pairs={{0,8},{8,16},{16,24},{24,32},{32,40},{40,48},{48,56},{56,64},{64,7... | collective-permute-start | bytes 786440 | tf_op jit(solution)/shard_map/while/body/eval_jaxpr/ppermute | solution.py:13
  19.9 3.3 %collective-permute-done = bf16[2,128,512]{2,1,0:T(8,128)(2,1)S(1)} collective-permute-done((bf16[2,128,512]{2,1,0:T(8,128)(2,1)S(1)}, bf16[2,128,512]{2,1,0:T(8,128)(2,1)S(1)}, u32[]{:S(2)}, u32[]{:S(2)}) %collective-permute-start) | collective-permute-done | bytes 262176 | tf_op jit(solution)/shard_map/while/body/eval_jaxpr/ppermute | solution.py:13
  24.0 6.5 %collective-permute-start = (bf16[2,128,512]{2,1,0:T(8,128)(2,1)S(1)}, bf16[2,128,512]{2,1,0:T(8,128)(2,1)S(1)}, u32[]{:S(2)}, u32[]{:S(2)}) collective-permute-start(bf16[2,128,512]{2,1,0:T(8,128)(2,1)S(1)} %get-tuple-element.472), channel_id=1, source_target_pairs={{0,8},{8,16},{16,24},{24,32},{32,40},{40,48},{48,56},{56,64},{64,7... | collective-permute-start | bytes 786440 | tf_op jit(solution)/shard_map/while/body/eval_jaxpr/ppermute | solution.py:13
  30.5 3.3 %collective-permute-done = bf16[2,128,512]{2,1,0:T(8,128)(2,1)S(1)} collective-permute-done((bf16[2,128,512]{2,1,0:T(8,128)(2,1)S(1)}, bf16[2,128,512]{2,1,0:T(8,128)(2,1)S(1)}, u32[]{:S(2)}, u32[]{:S(2)}) %collective-permute-start) | collective-permute-done | bytes 262176 | tf_op jit(solution)/shard_map/while/body/eval_jaxpr/ppermute | solution.py:13
  34.5 6.5 %collective-permute-start = (bf16[2,128,512]{2,1,0:T(8,128)(2,1)S(1)}, bf16[2,128,512]{2,1,0:T(8,128)(2,1)S(1)}, u32[]{:S(2)}, u32[]{:S(2)}) collective-permute-start(bf16[2,128,512]{2,1,0:T(8,128)(2,1)S(1)} %get-tuple-element.472), channel_id=1, source_target_pairs={{0,8},{8,16},{16,24},{24,32},{32,40},{40,48},{48,56},{56,64},{64,7... | collective-permute-start | bytes 786440 | tf_op jit(solution)/shard_map/while/body/eval_jaxpr/ppermute | solution.py:13
  41.0 3.3 %collective-permute-done = bf16[2,128,512]{2,1,0:T(8,128)(2,1)S(1)} collective-permute-done((bf16[2,128,512]{2,1,0:T(8,128)(2,1)S(1)}, bf16[2,128,512]{2,1,0:T(8,128)(2,1)S(1)}, u32[]{:S(2)}, u32[]{:S(2)}) %collective-permute-start) | collective-permute-done | bytes 262176 | tf_op jit(solution)/shard_map/while/body/eval_jaxpr/ppermute | solution.py:13
  45.0 6.5 %collective-permute-start = (bf16[2,128,512]{2,1,0:T(8,128)(2,1)S(1)}, bf16[2,128,512]{2,1,0:T(8,128)(2,1)S(1)}, u32[]{:S(2)}, u32[]{:S(2)}) collective-permute-start(bf16[2,128,512]{2,1,0:T(8,128)(2,1)S(1)} %get-tuple-element.472), channel_id=1, source_target_pairs={{0,8},{8,16},{16,24},{24,32},{32,40},{40,48},{48,56},{56,64},{64,7... | collective-permute-start | bytes 786440 | tf_op jit(solution)/shard_map/while/body/eval_jaxpr/ppermute | solution.py:13
  51.5 3.3 %collective-permute-done = bf16[2,128,512]{2,1,0:T(8,128)(2,1)S(1)} collective-permute-done((bf16[2,128,512]{2,1,0:T(8,128)(2,1)S(1)}, bf16[2,128,512]{2,1,0:T(8,128)(2,1)S(1)}, u32[]{:S(2)}, u32[]{:S(2)}) %collective-permute-start) | collective-permute-done | bytes 262176 | tf_op jit(solution)/shard_map/while/body/eval_jaxpr/ppermute | solution.py:13
  55.6 6.5 %collective-permute-start = (bf16[2,128,512]{2,1,0:T(8,128)(2,1)S(1)}, bf16[2,128,512]{2,1,0:T(8,128)(2,1)S(1)}, u32[]{:S(2)}, u32[]{:S(2)}) collective-permute-start(bf16[2,128,512]{2,1,0:T(8,128)(2,1)S(1)} %get-tuple-element.472), channel_id=1, source_target_pairs={{0,8},{8,16},{16,24},{24,32},{32,40},{40,48},{48,56},{56,64},{64,7... | collective-permute-start | bytes 786440 | tf_op jit(solution)/shard_map/while/body/eval_jaxpr/ppermute | solution.py:13
  62.0 3.3 %collective-permute-done = bf16[2,128,512]{2,1,0:T(8,128)(2,1)S(1)} collective-permute-done((bf16[2,128,512]{2,1,0:T(8,128)(2,1)S(1)}, bf16[2,128,512]{2,1,0:T(8,128)(2,1)S(1)}, u32[]{:S(2)}, u32[]{:S(2)}) %collective-permute-start) | collective-permute-done | bytes 262176 | tf_op jit(solution)/shard_map/while/body/eval_jaxpr/ppermute | solution.py:13
  66.1 6.5 %collective-permute-start = (bf16[2,128,512]{2,1,0:T(8,128)(2,1)S(1)}, bf16[2,128,512]{2,1,0:T(8,128)(2,1)S(1)}, u32[]{:S(2)}, u32[]{:S(2)}) collective-permute-start(bf16[2,128,512]{2,1,0:T(8,128)(2,1)S(1)} %get-tuple-element.472), channel_id=1, source_target_pairs={{0,8},{8,16},{16,24},{24,32},{32,40},{40,48},{48,56},{56,64},{64,7... | collective-permute-start | bytes 786440 | tf_op jit(solution)/shard_map/while/body/eval_jaxpr/ppermute | solution.py:13
  72.6 3.3 %collective-permute-done = bf16[2,128,512]{2,1,0:T(8,128)(2,1)S(1)} collective-permute-done((bf16[2,128,512]{2,1,0:T(8,128)(2,1)S(1)}, bf16[2,128,512]{2,1,0:T(8,128)(2,1)S(1)}, u32[]{:S(2)}, u32[]{:S(2)}) %collective-permute-start) | collective-permute-done | bytes 262176 | tf_op jit(solution)/shard_map/while/body/eval_jaxpr/ppermute | solution.py:13
  76.6 6.5 %collective-permute-start = (bf16[2,128,512]{2,1,0:T(8,128)(2,1)S(1)}, bf16[2,128,512]{2,1,0:T(8,128)(2,1)S(1)}, u32[]{:S(2)}, u32[]{:S(2)}) collective-permute-start(bf16[2,128,512]{2,1,0:T(8,128)(2,1)S(1)} %get-tuple-element.472), channel_id=1, source_target_pairs={{0,8},{8,16},{16,24},{24,32},{32,40},{40,48},{48,56},{56,64},{64,7... | collective-permute-start | bytes 786440 | tf_op jit(solution)/shard_map/while/body/eval_jaxpr/ppermute | solution.py:13
  83.1 3.3 %collective-permute-done = bf16[2,128,512]{2,1,0:T(8,128)(2,1)S(1)} collective-permute-done((bf16[2,128,512]{2,1,0:T(8,128)(2,1)S(1)}, bf16[2,128,512]{2,1,0:T(8,128)(2,1)S(1)}, u32[]{:S(2)}, u32[]{:S(2)}) %collective-permute-start) | collective-permute-done | bytes 262176 | tf_op jit(solution)/shard_map/while/body/eval_jaxpr/ppermute | solution.py:13
  87.1 1.7 pad_maximum_fusion.1
  92.5 1.7 broadcast.54
  94.3 69.4 %while.44 = (s32[]{:T(128)}, bf16[128,4096]{1,0:T(8,128)(2,1)}, f32[1152,512]{1,0:T(8,128)}, f32[1152,512]{1,0:T(8,128)S(1)}, bf16[1152,512]{1,0:T(8,128)(2,1)},...) while((s32[]{:T(128)}, bf16[128,4096]{1,0:T(8,128)(2,1)}, ...), condition=%wide.region_6.7_spmd.clone, body=%wide.region_2.6_spmd.clone.sunk | while | flops 1825243264 | bytes 54065528 | solution.py:90
  97.2 4.7 %exponential_reduce_fusion.2 = (f32[8,128]{1,0:T(8,128)S(1)}, f32[8,128,1152]{1,2,0:T(8,128)}) fusion(pred[128,1152]{0,1:T(8,128)(4,1)S(1)} %compare_and_fusion.2, bf16[128,8,128]{0,2,1:T(8,128)(2,1)S(1)} %bitcast.135, bf16[1152,512]{1,0:T(8,128)(2,1)} %get-tuple-element.519, s32[]{:T(128)S(6)} %select_n.58), kind=kOutput, calls=%fused_computation.12.clone.1 | convolution fusion | flops 306709632 | bytes 5427204 | tf_op jit(solution)/shard_map/while/body/eval_jaxpr/sub | solution.py:66
  101.9 3.1 %fusion.80 = bf16[8,128,1152]{1,2,0:T(8,128)(2,1)S(1)} fusion(f32[8,128]{1,0:T(8,128)S(1)} %get-tuple-element.465, f32[8,128,1152]{1,2,0:T(8,128)} %get-tuple-element.466), kind=kLoop, calls=%fused_computation.20.clone.1 | loop fusion | flops 2359296 | bytes 7081984 | tf_op jit(solution)/shard_map/while/body/eval_jaxpr/convert_element_type | solution.py:68
  114.5 4.7 %exponential_reduce_fusion.2 = (f32[8,128]{1,0:T(8,128)S(1)}, f32[8,128,1152]{1,2,0:T(8,128)}) fusion(pred[128,1152]{0,1:T(8,128)(4,1)S(1)} %compare_and_fusion.2, bf16[128,8,128]{0,2,1:T(8,128)(2,1)S(1)} %bitcast.135, bf16[1152,512]{1,0:T(8,128)(2,1)} %get-tuple-element.519, s32[]{:T(128)S(6)} %select_n.58), kind=kOutput, calls=%fused_computation.12.clone.1 | convolution fusion | flops 306709632 | bytes 5427204 | tf_op jit(solution)/shard_map/while/body/eval_jaxpr/sub | solution.py:66
  119.3 3.1 %fusion.80 = bf16[8,128,1152]{1,2,0:T(8,128)(2,1)S(1)} fusion(f32[8,128]{1,0:T(8,128)S(1)} %get-tuple-element.465, f32[8,128,1152]{1,2,0:T(8,128)} %get-tuple-element.466), kind=kLoop, calls=%fused_computation.20.clone.1 | loop fusion | flops 2359296 | bytes 7081984 | tf_op jit(solution)/shard_map/while/body/eval_jaxpr/convert_element_type | solution.py:68
  126.4 1.7 fusion.83
  131.9 4.7 %exponential_reduce_fusion.2 = (f32[8,128]{1,0:T(8,128)S(1)}, f32[8,128,1152]{1,2,0:T(8,128)}) fusion(pred[128,1152]{0,1:T(8,128)(4,1)S(1)} %compare_and_fusion.2, bf16[128,8,128]{0,2,1:T(8,128)(2,1)S(1)} %bitcast.135, bf16[1152,512]{1,0:T(8,128)(2,1)} %get-tuple-element.519, s32[]{:T(128)S(6)} %select_n.58), kind=kOutput, calls=%fused_computation.12.clone.1 | convolution fusion | flops 306709632 | bytes 5427204 | tf_op jit(solution)/shard_map/while/body/eval_jaxpr/sub | solution.py:66
  136.6 3.1 %fusion.80 = bf16[8,128,1152]{1,2,0:T(8,128)(2,1)S(1)} fusion(f32[8,128]{1,0:T(8,128)S(1)} %get-tuple-element.465, f32[8,128,1152]{1,2,0:T(8,128)} %get-tuple-element.466), kind=kLoop, calls=%fused_computation.20.clone.1 | loop fusion | flops 2359296 | bytes 7081984 | tf_op jit(solution)/shard_map/while/body/eval_jaxpr/convert_element_type | solution.py:68
  149.2 4.7 %exponential_reduce_fusion.2 = (f32[8,128]{1,0:T(8,128)S(1)}, f32[8,128,1152]{1,2,0:T(8,128)}) fusion(pred[128,1152]{0,1:T(8,128)(4,1)S(1)} %compare_and_fusion.2, bf16[128,8,128]{0,2,1:T(8,128)(2,1)S(1)} %bitcast.135, bf16[1152,512]{1,0:T(8,128)(2,1)} %get-tuple-element.519, s32[]{:T(128)S(6)} %select_n.58), kind=kOutput, calls=%fused_computation.12.clone.1 | convolution fusion | flops 306709632 | bytes 5427204 | tf_op jit(solution)/shard_map/while/body/eval_jaxpr/sub | solution.py:66
  154.0 3.1 %fusion.80 = bf16[8,128,1152]{1,2,0:T(8,128)(2,1)S(1)} fusion(f32[8,128]{1,0:T(8,128)S(1)} %get-tuple-element.465, f32[8,128,1152]{1,2,0:T(8,128)} %get-tuple-element.466), kind=kLoop, calls=%fused_computation.20.clone.1 | loop fusion | flops 2359296 | bytes 7081984 | tf_op jit(solution)/shard_map/while/body/eval_jaxpr/convert_element_type | solution.py:68
  161.2 1.7 fusion.83
  165.5 2.6 pad_maximum_fusion
  168.1 110.7 %while.43 = (s32[]{:T(128)}, f32[2,128,512]{2,1,0:T(8,128)S(1)}, f32[8,2,128,512]{3,2,1,0:T(8,128)}, s32[]{:T(128)}) while((s32[]{:T(128)}, f32[2,128,512]{2,1,0:T(8,128)S(1)}, f32[8,2,128,512]{3,2,1,0:T(8,128)}, s32[]{:T(128)}) %tuple.83), condition=%wide.region_8.9_spmd, body=%wide.region_7.8_spmd.sunk | while | flops 131074 | bytes 3670121 | solution.py:100
  168.1 1.9 collective-permute-start.1
  170.0 11.4 %collective-permute-done.1 = f32[2,128,512]{2,1,0:T(8,128)S(1)} collective-permute-done((f32[2,128,512]{2,1,0:T(8,128)S(1)}, f32[2,128,512]{2,1,0:T(8,128)S(1)}, u32[]{:S(2)}, u32[]{:S(2)}) %collective-permute-start.1) | collective-permute-done | bytes 524320 | tf_op jit(solution)/shard_map/while/body/eval_jaxpr/ppermute | solution.py:13
  182.5 1.9 collective-permute-start.1
  184.5 10.7 %collective-permute-done.1 = f32[2,128,512]{2,1,0:T(8,128)S(1)} collective-permute-done((f32[2,128,512]{2,1,0:T(8,128)S(1)}, f32[2,128,512]{2,1,0:T(8,128)S(1)}, u32[]{:S(2)}, u32[]{:S(2)}) %collective-permute-start.1) | collective-permute-done | bytes 524320 | tf_op jit(solution)/shard_map/while/body/eval_jaxpr/ppermute | solution.py:13
  196.3 1.9 collective-permute-start.1
  198.2 10.7 %collective-permute-done.1 = f32[2,128,512]{2,1,0:T(8,128)S(1)} collective-permute-done((f32[2,128,512]{2,1,0:T(8,128)S(1)}, f32[2,128,512]{2,1,0:T(8,128)S(1)}, u32[]{:S(2)}, u32[]{:S(2)}) %collective-permute-start.1) | collective-permute-done | bytes 524320 | tf_op jit(solution)/shard_map/while/body/eval_jaxpr/ppermute | solution.py:13
  210.0 1.9 collective-permute-start.1
  212.0 10.7 %collective-permute-done.1 = f32[2,128,512]{2,1,0:T(8,128)S(1)} collective-permute-done((f32[2,128,512]{2,1,0:T(8,128)S(1)}, f32[2,128,512]{2,1,0:T(8,128)S(1)}, u32[]{:S(2)}, u32[]{:S(2)}) %collective-permute-start.1) | collective-permute-done | bytes 524320 | tf_op jit(solution)/shard_map/while/body/eval_jaxpr/ppermute | solution.py:13
  223.8 1.9 collective-permute-start.1
  225.7 10.7 %collective-permute-done.1 = f32[2,128,512]{2,1,0:T(8,128)S(1)} collective-permute-done((f32[2,128,512]{2,1,0:T(8,128)S(1)}, f32[2,128,512]{2,1,0:T(8,128)S(1)}, u32[]{:S(2)}, u32[]{:S(2)}) %collective-permute-start.1) | collective-permute-done | bytes 524320 | tf_op jit(solution)/shard_map/while/body/eval_jaxpr/ppermute | solution.py:13
  237.5 1.9 collective-permute-start.1
  239.5 10.7 %collective-permute-done.1 = f32[2,128,512]{2,1,0:T(8,128)S(1)} collective-permute-done((f32[2,128,512]{2,1,0:T(8,128)S(1)}, f32[2,128,512]{2,1,0:T(8,128)S(1)}, u32[]{:S(2)}, u32[]{:S(2)}) %collective-permute-start.1) | collective-permute-done | bytes 524320 | tf_op jit(solution)/shard_map/while/body/eval_jaxpr/ppermute | solution.py:13
  251.3 1.9 collective-permute-start.1
  253.2 10.7 %collective-permute-done.1 = f32[2,128,512]{2,1,0:T(8,128)S(1)} collective-permute-done((f32[2,128,512]{2,1,0:T(8,128)S(1)}, f32[2,128,512]{2,1,0:T(8,128)S(1)}, u32[]{:S(2)}, u32[]{:S(2)}) %collective-permute-start.1) | collective-permute-done | bytes 524320 | tf_op jit(solution)/shard_map/while/body/eval_jaxpr/ppermute | solution.py:13
  265.0 1.9 collective-permute-start.1
  267.0 10.7 %collective-permute-done.1 = f32[2,128,512]{2,1,0:T(8,128)S(1)} collective-permute-done((f32[2,128,512]{2,1,0:T(8,128)S(1)}, f32[2,128,512]{2,1,0:T(8,128)S(1)}, u32[]{:S(2)}, u32[]{:S(2)}) %collective-permute-start.1) | collective-permute-done | bytes 524320 | tf_op jit(solution)/shard_map/while/body/eval_jaxpr/ppermute | solution.py:13
  (111 shorter events, 61.1 us)
Async XLA Ops:
  6.5 6.2 %collective-permute-start = (bf16[2,128,512]{2,1,0:T(8,128)(2,1)S(1)}, bf16[2,128,512]{2,1,0:T(8,128)(2,1)S(1)}, u32[]{:S(2)}, u32[]{:S(2)}) collective-permute-start(bf16[2,128,512]{2,1,0:T(8,128)(2,1)S(1)} %get-tuple-element.472), channel_id=1, source_target_pairs={{0,8},{8,16},{16,24},{24,32},{32,40},{40,48},{48,56},{56,64},{64,7... | collective-permute-start | bytes 786440 | tf_op jit(solution)/shard_map/while/body/eval_jaxpr/ppermute | solution.py:13
  13.4 9.8 %collective-permute-start = (bf16[2,128,512]{2,1,0:T(8,128)(2,1)S(1)}, bf16[2,128,512]{2,1,0:T(8,128)(2,1)S(1)}, u32[]{:S(2)}, u32[]{:S(2)}) collective-permute-start(bf16[2,128,512]{2,1,0:T(8,128)(2,1)S(1)} %get-tuple-element.472), channel_id=1, source_target_pairs={{0,8},{8,16},{16,24},{24,32},{32,40},{40,48},{48,56},{56,64},{64,7... | collective-permute-start | bytes 786440 | tf_op jit(solution)/shard_map/while/body/eval_jaxpr/ppermute | solution.py:13
  24.0 9.8 %collective-permute-start = (bf16[2,128,512]{2,1,0:T(8,128)(2,1)S(1)}, bf16[2,128,512]{2,1,0:T(8,128)(2,1)S(1)}, u32[]{:S(2)}, u32[]{:S(2)}) collective-permute-start(bf16[2,128,512]{2,1,0:T(8,128)(2,1)S(1)} %get-tuple-element.472), channel_id=1, source_target_pairs={{0,8},{8,16},{16,24},{24,32},{32,40},{40,48},{48,56},{56,64},{64,7... | collective-permute-start | bytes 786440 | tf_op jit(solution)/shard_map/while/body/eval_jaxpr/ppermute | solution.py:13
  34.5 9.8 %collective-permute-start = (bf16[2,128,512]{2,1,0:T(8,128)(2,1)S(1)}, bf16[2,128,512]{2,1,0:T(8,128)(2,1)S(1)}, u32[]{:S(2)}, u32[]{:S(2)}) collective-permute-start(bf16[2,128,512]{2,1,0:T(8,128)(2,1)S(1)} %get-tuple-element.472), channel_id=1, source_target_pairs={{0,8},{8,16},{16,24},{24,32},{32,40},{40,48},{48,56},{56,64},{64,7... | collective-permute-start | bytes 786440 | tf_op jit(solution)/shard_map/while/body/eval_jaxpr/ppermute | solution.py:13
  45.0 9.8 %collective-permute-start = (bf16[2,128,512]{2,1,0:T(8,128)(2,1)S(1)}, bf16[2,128,512]{2,1,0:T(8,128)(2,1)S(1)}, u32[]{:S(2)}, u32[]{:S(2)}) collective-permute-start(bf16[2,128,512]{2,1,0:T(8,128)(2,1)S(1)} %get-tuple-element.472), channel_id=1, source_target_pairs={{0,8},{8,16},{16,24},{24,32},{32,40},{40,48},{48,56},{56,64},{64,7... | collective-permute-start | bytes 786440 | tf_op jit(solution)/shard_map/while/body/eval_jaxpr/ppermute | solution.py:13
  55.6 9.8 %collective-permute-start = (bf16[2,128,512]{2,1,0:T(8,128)(2,1)S(1)}, bf16[2,128,512]{2,1,0:T(8,128)(2,1)S(1)}, u32[]{:S(2)}, u32[]{:S(2)}) collective-permute-start(bf16[2,128,512]{2,1,0:T(8,128)(2,1)S(1)} %get-tuple-element.472), channel_id=1, source_target_pairs={{0,8},{8,16},{16,24},{24,32},{32,40},{40,48},{48,56},{56,64},{64,7... | collective-permute-start | bytes 786440 | tf_op jit(solution)/shard_map/while/body/eval_jaxpr/ppermute | solution.py:13
  66.1 9.8 %collective-permute-start = (bf16[2,128,512]{2,1,0:T(8,128)(2,1)S(1)}, bf16[2,128,512]{2,1,0:T(8,128)(2,1)S(1)}, u32[]{:S(2)}, u32[]{:S(2)}) collective-permute-start(bf16[2,128,512]{2,1,0:T(8,128)(2,1)S(1)} %get-tuple-element.472), channel_id=1, source_target_pairs={{0,8},{8,16},{16,24},{24,32},{32,40},{40,48},{48,56},{56,64},{64,7... | collective-permute-start | bytes 786440 | tf_op jit(solution)/shard_map/while/body/eval_jaxpr/ppermute | solution.py:13
  76.6 9.8 %collective-permute-start = (bf16[2,128,512]{2,1,0:T(8,128)(2,1)S(1)}, bf16[2,128,512]{2,1,0:T(8,128)(2,1)S(1)}, u32[]{:S(2)}, u32[]{:S(2)}) collective-permute-start(bf16[2,128,512]{2,1,0:T(8,128)(2,1)S(1)} %get-tuple-element.472), channel_id=1, source_target_pairs={{0,8},{8,16},{16,24},{24,32},{32,40},{40,48},{48,56},{56,64},{64,7... | collective-permute-start | bytes 786440 | tf_op jit(solution)/shard_map/while/body/eval_jaxpr/ppermute | solution.py:13
  101.9 3.1 %copy-start.1 = (bf16[1152,512]{1,0:T(8,128)(2,1)S(1)}, bf16[1152,512]{1,0:T(8,128)(2,1)}, u32[]{:S(2)}) copy-start(bf16[1152,512]{1,0:T(8,128)(2,1)} %get-tuple-element.521) | copy-start | bytes 3538948 | tf_op jit(solution)/shard_map/while
  101.9 4.5 %slice-start = ((s8[4718592]{0:T(1024)(128)(4,1)}), s8[4194304]{0:T(1024)(128)(4,1)S(1)}, s32[]{:S(2)}) async-start(s8[4718592]{0:T(1024)(128)(4,1)} %bitcast.130), calls=%async_computation | async-start | bytes 8388608 | tf_op jit(solution)/shard_map/while
  105.0 1.4 slice-start.1
  119.2 3.1 %copy-start.1 = (bf16[1152,512]{1,0:T(8,128)(2,1)S(1)}, bf16[1152,512]{1,0:T(8,128)(2,1)}, u32[]{:S(2)}) copy-start(bf16[1152,512]{1,0:T(8,128)(2,1)} %get-tuple-element.521) | copy-start | bytes 3538948 | tf_op jit(solution)/shard_map/while
  119.2 4.5 %slice-start = ((s8[4718592]{0:T(1024)(128)(4,1)}), s8[4194304]{0:T(1024)(128)(4,1)S(1)}, s32[]{:S(2)}) async-start(s8[4718592]{0:T(1024)(128)(4,1)} %bitcast.130), calls=%async_computation | async-start | bytes 8388608 | tf_op jit(solution)/shard_map/while
  122.4 1.4 slice-start.1
  136.6 3.1 %copy-start.1 = (bf16[1152,512]{1,0:T(8,128)(2,1)S(1)}, bf16[1152,512]{1,0:T(8,128)(2,1)}, u32[]{:S(2)}) copy-start(bf16[1152,512]{1,0:T(8,128)(2,1)} %get-tuple-element.521) | copy-start | bytes 3538948 | tf_op jit(solution)/shard_map/while
  136.6 4.5 %slice-start = ((s8[4718592]{0:T(1024)(128)(4,1)}), s8[4194304]{0:T(1024)(128)(4,1)S(1)}, s32[]{:S(2)}) async-start(s8[4718592]{0:T(1024)(128)(4,1)} %bitcast.130), calls=%async_computation | async-start | bytes 8388608 | tf_op jit(solution)/shard_map/while
  139.7 1.4 slice-start.1
  154.0 3.1 %copy-start.1 = (bf16[1152,512]{1,0:T(8,128)(2,1)S(1)}, bf16[1152,512]{1,0:T(8,128)(2,1)}, u32[]{:S(2)}) copy-start(bf16[1152,512]{1,0:T(8,128)(2,1)} %get-tuple-element.521) | copy-start | bytes 3538948 | tf_op jit(solution)/shard_map/while
  154.0 4.5 %slice-start = ((s8[4718592]{0:T(1024)(128)(4,1)}), s8[4194304]{0:T(1024)(128)(4,1)S(1)}, s32[]{:S(2)}) async-start(s8[4718592]{0:T(1024)(128)(4,1)} %bitcast.130), calls=%async_computation | async-start | bytes 8388608 | tf_op jit(solution)/shard_map/while
  157.1 1.4 slice-start.1
  163.7 1.7 copy-start
  168.1 13.3 %collective-permute-start.1 = (f32[2,128,512]{2,1,0:T(8,128)S(1)}, f32[2,128,512]{2,1,0:T(8,128)S(1)}, u32[]{:S(2)}, u32[]{:S(2)}) collective-permute-start(f32[2,128,512]{2,1,0:T(8,128)S(1)} %get-tuple-element.538), channel_id=1, source_target_pairs={{8,0},{16,8},{24,16},{32,24},{40,32},{48,40},{56,48},{64,56},{72,6... | collective-permute-start | bytes 1572872 | tf_op jit(solution)/shard_map/while/body/eval_jaxpr/ppermute | solution.py:13
  182.5 12.6 %collective-permute-start.1 = (f32[2,128,512]{2,1,0:T(8,128)S(1)}, f32[2,128,512]{2,1,0:T(8,128)S(1)}, u32[]{:S(2)}, u32[]{:S(2)}) collective-permute-start(f32[2,128,512]{2,1,0:T(8,128)S(1)} %get-tuple-element.538), channel_id=1, source_target_pairs={{8,0},{16,8},{24,16},{32,24},{40,32},{48,40},{56,48},{64,56},{72,6... | collective-permute-start | bytes 1572872 | tf_op jit(solution)/shard_map/while/body/eval_jaxpr/ppermute | solution.py:13
  196.3 12.6 %collective-permute-start.1 = (f32[2,128,512]{2,1,0:T(8,128)S(1)}, f32[2,128,512]{2,1,0:T(8,128)S(1)}, u32[]{:S(2)}, u32[]{:S(2)}) collective-permute-start(f32[2,128,512]{2,1,0:T(8,128)S(1)} %get-tuple-element.538), channel_id=1, source_target_pairs={{8,0},{16,8},{24,16},{32,24},{40,32},{48,40},{56,48},{64,56},{72,6... | collective-permute-start | bytes 1572872 | tf_op jit(solution)/shard_map/while/body/eval_jaxpr/ppermute | solution.py:13
  210.0 12.6 %collective-permute-start.1 = (f32[2,128,512]{2,1,0:T(8,128)S(1)}, f32[2,128,512]{2,1,0:T(8,128)S(1)}, u32[]{:S(2)}, u32[]{:S(2)}) collective-permute-start(f32[2,128,512]{2,1,0:T(8,128)S(1)} %get-tuple-element.538), channel_id=1, source_target_pairs={{8,0},{16,8},{24,16},{32,24},{40,32},{48,40},{56,48},{64,56},{72,6... | collective-permute-start | bytes 1572872 | tf_op jit(solution)/shard_map/while/body/eval_jaxpr/ppermute | solution.py:13
  223.8 12.6 %collective-permute-start.1 = (f32[2,128,512]{2,1,0:T(8,128)S(1)}, f32[2,128,512]{2,1,0:T(8,128)S(1)}, u32[]{:S(2)}, u32[]{:S(2)}) collective-permute-start(f32[2,128,512]{2,1,0:T(8,128)S(1)} %get-tuple-element.538), channel_id=1, source_target_pairs={{8,0},{16,8},{24,16},{32,24},{40,32},{48,40},{56,48},{64,56},{72,6... | collective-permute-start | bytes 1572872 | tf_op jit(solution)/shard_map/while/body/eval_jaxpr/ppermute | solution.py:13
  237.5 12.6 %collective-permute-start.1 = (f32[2,128,512]{2,1,0:T(8,128)S(1)}, f32[2,128,512]{2,1,0:T(8,128)S(1)}, u32[]{:S(2)}, u32[]{:S(2)}) collective-permute-start(f32[2,128,512]{2,1,0:T(8,128)S(1)} %get-tuple-element.538), channel_id=1, source_target_pairs={{8,0},{16,8},{24,16},{32,24},{40,32},{48,40},{56,48},{64,56},{72,6... | collective-permute-start | bytes 1572872 | tf_op jit(solution)/shard_map/while/body/eval_jaxpr/ppermute | solution.py:13
  251.3 12.6 %collective-permute-start.1 = (f32[2,128,512]{2,1,0:T(8,128)S(1)}, f32[2,128,512]{2,1,0:T(8,128)S(1)}, u32[]{:S(2)}, u32[]{:S(2)}) collective-permute-start(f32[2,128,512]{2,1,0:T(8,128)S(1)} %get-tuple-element.538), channel_id=1, source_target_pairs={{8,0},{16,8},{24,16},{32,24},{40,32},{48,40},{56,48},{64,56},{72,6... | collective-permute-start | bytes 1572872 | tf_op jit(solution)/shard_map/while/body/eval_jaxpr/ppermute | solution.py:13
  265.0 12.6 %collective-permute-start.1 = (f32[2,128,512]{2,1,0:T(8,128)S(1)}, f32[2,128,512]{2,1,0:T(8,128)S(1)}, u32[]{:S(2)}, u32[]{:S(2)}) collective-permute-start(f32[2,128,512]{2,1,0:T(8,128)S(1)} %get-tuple-element.538), channel_id=1, source_target_pairs={{8,0},{16,8},{24,16},{32,24},{40,32},{48,40},{56,48},{64,56},{72,6... | collective-permute-start | bytes 1572872 | tf_op jit(solution)/shard_map/while/body/eval_jaxpr/ppermute | solution.py:13
where the time goes:
time: 281 us; the launch traced here: 280 us
  waiting for transfers between devices  113 us (40%)
  starting transfers between devices  63.6 us (23%)
  matrix products  41.6 us (15%)
  other arithmetic  33.4 us (12%)
  local copies, waits for them, and re-layouts  27 us (10%)
    ppermute x16, waiting for transfers between devices, passed_along(): return lax.ppermute(x, axis, pairs)  113 us
    ppermute x16, starting transfers between devices, passed_along(): return lax.ppermute(x, axis, pairs)  63.6 us
    sub x4, matrix products, per_group(): expo = jnp.exp(scores - peak)  19 us
    convert_element_type x4, other arithmetic, per_group(): probs_b = probs.astype(jnp.bfloat16)  12.4 us
    add x8, other arithmetic, backward_step(): return (moved + term, None)  8.96 us
    dot_general x4, matrix products, per_group(): jnp.einsum('gtk,tgd->kd', dscores, q_block, preferred_element_type=jnp.fl...  6.69 us
    dot_general x4, matrix products, per_group(): jnp.einsum('gtk,kd->tgd', dscores, k_block, preferred_element_type=jnp.fl...  6.08 us
    dynamic_update_slice x8, local copies, waits for them, and re-layouts, per_device(): last, later = lax.scan(forward_step, stacked, None, length=RADIUS)  5.75 us
  transfers between devices with their start and end apart: 16, of which 16 were waited for; matrix products, arithmetic and copies ran while one was open for 0% of the time, Pallas kernels for 0%

commit v1 on v0

v1 whole, which is shorter than its diff:
```python
import functools
import math

import jax
import jax.numpy as jnp
from jax import lax
from jax.experimental import pallas as pl
from jax.experimental.pallas import tpu as pltpu
from jax.sharding import PartitionSpec as P

HD = 128
BT = 256
ND = 5
G = 8
FAR = ND - 1
NEG = -1e30
F32 = jnp.float32
BF16 = jnp.bfloat16
MESH = pl.DeviceIdType.MESH


def dot(a, b, ca, cb):
    return lax.dot_general(
        a, b, (((ca,), (cb,)), ((), ())), preferred_element_type=F32
    )


def kernel(
    chips, q_hbm, k_hbm, v_hbm, seg_ref, mask_ref, do_hbm,
    dq_out, gk_out, gv_out,
    q_s, o_s, kv_s, bias_s, e_s, dp_s, ds_s, p_s, kt_s, m_s, l_s, dl_s,
    rbuf, sbuf, gacc, gout, dq_s, mk_s,
    f_recv, f_own, f_relay, f_xsend, f_loc,
    q_recv, q_send, q_loc, k_recv, k_send,
    b_recv, b_send, dq_recv, dq_send, dq_loc, g_recv, g_send, g_loc,
):
    me = lax.axis_index("cp")
    core = me % 2
    chip = me // 2
    other = 1 - core
    partner = chip * 2 + other
    after = (chip + 1) % chips
    before = (chip + chips - 1) % chips
    scale = HD ** -0.5
    mine = pl.ds(pl.multiple_of(core * 128, 128), 128)
    theirs = pl.ds(pl.multiple_of(other * 128, 128), 128)

    barrier = pltpu.get_barrier_semaphore()
    for peer in (partner, after * 2, after * 2 + 1, before * 2, before * 2 + 1):
        pl.semaphore_signal(barrier, inc=1, device_id={"cp": peer}, device_id_type=MESH)
    pl.semaphore_wait(barrier, 5)

    def remote(src, dst, ssem, rsem, cp):
        return pltpu.make_async_remote_copy(
            src_ref=src, dst_ref=dst, send_sem=ssem, recv_sem=rsem,
            device_id={"cp": cp}, device_id_type=MESH,
        )

    def columns(first, count=1):
        return pl.ds(pl.multiple_of(first * 128, 128), count * 128)

    srcs = (k_hbm, v_hbm)

    def own_send(hl, kv, b):
        return remote(
            srcs[kv].at[:, columns(2 * b + hl)], kv_s.at[hl, kv, 1, mine, :],
            f_own.at[hl, kv, b], f_recv.at[hl, kv, 1, core], after * 2 + b,
        )

    def x_send(hl, kv):
        return remote(
            srcs[kv].at[:, columns(2 * other + hl)], kv_s.at[hl, kv, 0, mine, :],
            f_xsend.at[hl, kv], f_recv.at[hl, kv, 0, core], partner,
        )

    def x_recv(hl, kv):
        return remote(
            srcs[kv].at[:, columns(2 * other + hl)], kv_s.at[hl, kv, 0, theirs, :],
            f_xsend.at[hl, kv], f_recv.at[hl, kv, 0, other], partner,
        )

    def local_kv(hl, kv):
        return pltpu.make_async_copy(
            srcs[kv].at[:, columns(2 * core + hl)], kv_s.at[hl, kv, 0, mine, :],
            f_loc.at[hl, kv],
        )

    def half(i):
        return pl.ds(i * 128, 128)

    def hop(hl, kv, d, i):
        return remote(
            kv_s.at[hl, kv, d, half(i), :], kv_s.at[hl, kv, d + 1, half(i), :],
            f_relay.at[hl, kv, d - 1, i], f_recv.at[hl, kv, d + 1, i],
            after * 2 + core,
        )

    def hop_recv(hl, kv, d, i):
        return remote(
            kv_s.at[hl, kv, d, half(i), :], kv_s.at[hl, kv, d, half(i), :],
            f_relay.at[hl, kv, 0, i], f_recv.at[hl, kv, d, i],
            after * 2 + core,
        )

    heads = (q_hbm, do_hbm)
    held = (q_s, o_s)

    def qo_send(t, i):
        hl = i // G
        return remote(
            heads[t].at[:, columns(other * 16 + i)], held[t].at[i, mine, :],
            q_send.at[t, hl], q_recv.at[t, hl], partner,
        )

    def qo_local(t, i):
        return pltpu.make_async_copy(
            heads[t].at[:, columns(core * 16 + i)], held[t].at[i, mine, :],
            q_loc.at[t, i // G],
        )

    def qo_wait(t, hl):
        rows = held[t].at[hl * G:(hl + 1) * G, theirs, :]
        remote(rows, rows, q_send.at[t, hl], q_recv.at[t, hl], partner).wait_recv()
        own = held[t].at[hl * G:(hl + 1) * G, mine, :]
        pltpu.make_async_copy(own, own, q_loc.at[t, hl]).wait()

    def qo_wait_send(t, hl):
        rows = held[t].at[hl * G:(hl + 1) * G, theirs, :]
        remote(rows, rows, q_send.at[t, hl], q_recv.at[t, hl], partner).wait_send()

    mask_copy = remote(mask_ref, mk_s.at[core], k_send, k_recv, partner)
    mask_back = remote(mask_ref, mk_s.at[other], k_send, k_recv, partner)

    for kv in range(2):
        for b in range(2):
            own_send(0, kv, b).start()
    for kv in range(2):
        x_send(0, kv).start()
        local_kv(0, kv).start()
    mask_copy.start()
    for t in range(2):
        for i in range(G):
            qo_send(t, i).start()
            qo_local(t, i).start()

    first = 2 * chip - 2 * FAR

    def seg_row(j):
        return seg_ref[pl.ds((first + j + 2 * chips) % (2 * chips), 1), :].astype(F32)

    q_seg = jnp.concatenate([seg_row(2 * FAR), seg_row(2 * FAR + 1)], axis=1)
    q_at = lax.broadcasted_iota(jnp.int32, (128, BT), 1)
    k_at = lax.broadcasted_iota(jnp.int32, (128, BT), 0)
    for j in range(2 * ND):
        row = jnp.broadcast_to(seg_row(j), (128, 128))
        col = jnp.concatenate([row.T] * 2, axis=1)
        offset = (j - 2 * FAR) * 128
        ok = (col == q_seg) & (k_at + offset <= q_at) & (k_at + (first + j) * 128 >= 0)
        bias_s[FAR - j // 2, (j % 2) * 128:(j % 2) * 128 + 128, :] = jnp.where(ok, 0.0, NEG)

    mk_s[pl.ds(core, 1), :, :] = mask_ref[...][None]
    mask_back.wait_recv()
    mask_col = jnp.concatenate(
        [jnp.broadcast_to(mk_s[i].astype(F32), (128, 128)).T for i in range(2)], axis=0
    ).astype(BF16)

    def mask_grad(hl):
        def body(i, carry):
            o_s[hl * G + i] = o_s[hl * G + i] * mask_col
            return carry
        lax.fori_loop(0, G, body, 0)

    def arrive(hl, d):
        for kv in range(2):
            if d == 0:
                local_kv(hl, kv).wait()
                x_recv(hl, kv).wait_recv()
            else:
                for i in range(2):
                    hop_recv(hl, kv, d, i).wait_recv()
                    if d < FAR:
                        hop(hl, kv, d, i).start()

    c2 = scale * math.log2(math.e)

    def pass1(hl, d):
        def body(g, carry):
            s = dot(kv_s[hl, 0, d], q_s[hl * G + g], 1, 1)
            dp = dot(kv_s[hl, 1, d], o_s[hl * G + g], 1, 1)
            x = s * c2 + bias_s[d]
            peak = jnp.max(x, axis=0, keepdims=True)
            if d > 0:
                old = m_s[d - 1, g]
                peak = jnp.maximum(old, peak)
            e = jnp.exp2(x - peak)
            total = jnp.sum(e, axis=0, keepdims=True)
            inner = jnp.sum(e * dp, axis=0, keepdims=True)
            if d > 0:
                fade = jnp.exp2(old - peak)
                total = total + l_s[g] * fade
                inner = inner + dl_s[g] * fade
            m_s[d, g] = peak
            l_s[g] = total
            dl_s[g] = inner
            e_s[g, d] = e
            dp_s[g, d] = dp
            return carry
        lax.fori_loop(0, G, body, 0)

    def pass2(hl, d):
        def body(g, carry):
            inv = 1.0 / l_s[g]
            f = jnp.exp2(m_s[d, g] - m_s[FAR, g]) * inv
            delta = dl_s[g] * inv
            p = e_s[g, d] * f
            p_s[g] = p.astype(BF16)
            ds_s[g, d * BT:(d + 1) * BT, :] = (p * (dp_s[g, d] - delta)).astype(BF16)
            return carry
        lax.fori_loop(0, G, body, 0)
        span = slice(hl * G, (hl + 1) * G)
        ds = jnp.concatenate([ds_s[g, d * BT:(d + 1) * BT, :] for g in range(G)], axis=1)
        gacc[hl, 0, d] = dot(ds, q_s[span].reshape(G * BT, HD), 1, 0)
        p = jnp.concatenate([p_s[g] for g in range(G)], axis=1)
        gacc[hl, 1, d] = dot(p, o_s[span].reshape(G * BT, HD), 1, 0)

    def transposed_keys(hl):
        for d in range(ND):
            kt_s[:, d * BT:(d + 1) * BT] = kv_s[hl, 0, d].astype(F32).T.astype(BF16)

    def grad_q(hl):
        def body(g, carry):
            dqt = dot(kt_s[...], ds_s[g], 1, 0) * scale
            dq_s[:, columns(hl * G + g)] = dqt.T.astype(BF16)
            return carry
        lax.fori_loop(0, G, body, 0)

    def dq_copy(hl):
        return pltpu.make_async_copy(
            dq_s.at[mine, columns(hl * G, G)],
            dq_out.at[:, columns(core * 16 + hl * G, G)], dq_loc.at[hl],
        )

    def dq_give(hl):
        return remote(
            dq_s.at[theirs, columns(hl * G, G)],
            dq_out.at[:, columns(core * 16 + hl * G, G)],
            dq_send.at[hl], dq_recv.at[hl], partner,
        )

    def dq_take(hl):
        return remote(
            dq_s.at[theirs, columns(hl * G, G)],
            dq_out.at[:, columns(other * 16 + hl * G, G)],
            dq_send.at[hl], dq_recv.at[hl], partner,
        )

    def back(hl, kv, d, i):
        return remote(
            sbuf.at[hl, kv, d - 1, half(i), :], rbuf.at[hl, kv, d - 1, half(i), :],
            b_send.at[hl, kv, d - 1, i], b_recv.at[hl, kv, d - 1, i],
            before * 2 + core,
        )

    outs = (gk_out, gv_out)

    def g_copy(hl, kv):
        return pltpu.make_async_copy(
            gout.at[hl, kv, mine, :], outs[kv].at[:, columns(2 * core + hl)],
            g_loc.at[hl, kv],
        )

    def g_give(hl, kv):
        return remote(
            gout.at[hl, kv, theirs, :], outs[kv].at[:, columns(2 * core + hl)],
            g_send.at[hl, kv], g_recv.at[hl, kv], partner,
        )

    def g_take(hl, kv):
        return remote(
            gout.at[hl, kv, theirs, :], outs[kv].at[:, columns(2 * other + hl)],
            g_send.at[hl, kv], g_recv.at[hl, kv], partner,
        )

    def chain(hl, d):
        for kv in range(2):
            for i in range(2):
                rows = slice(i * 128, i * 128 + 128)
                part = gacc[hl, kv, d, rows, :]
                if d < FAR:
                    back(hl, kv, d + 1, i).wait_recv()
                    part = part + rbuf[hl, kv, d, rows, :].astype(F32)
                if d > 0:
                    sbuf[hl, kv, d - 1, rows, :] = part.astype(BF16)
                    back(hl, kv, d, i).start()
                else:
                    if kv == 0:
                        part = part * scale
                    gout[hl, kv, rows, :] = part.astype(BF16)
            if d == 0:
                g_give(hl, kv).start()
                g_copy(hl, kv).start()

    def start_second():
        for kv in range(2):
            for b in range(2):
                own_send(1, kv, b).start()
        for kv in range(2):
            x_send(1, kv).start()
            local_kv(1, kv).start()
        for t in range(2):
            for i in range(G, 2 * G):
                qo_send(t, i).start()
                qo_local(t, i).start()

    qo_wait(0, 0)
    qo_wait(1, 0)
    mask_grad(0)
    for d in range(ND):
        arrive(0, d)
        if d == FAR - 1:
            start_second()
        pass1(0, d)
    pass2(0, 4)
    chain(0, 4)
    arrive(1, 0)
    arrive(1, 1)
    pass2(0, 3)
    pass2(0, 2)
    arrive(1, 2)
    chain(0, 3)
    pass2(0, 1)
    pass2(0, 0)
    arrive(1, 3)
    chain(0, 2)
    transposed_keys(0)
    grad_q(0)
    dq_give(0).start()
    dq_copy(0).start()
    qo_wait(0, 1)
    qo_wait(1, 1)
    mask_grad(1)
    pass1(1, 0)
    chain(0, 1)
    pass1(1, 1)
    pass1(1, 2)
    chain(0, 0)
    pass1(1, 3)
    arrive(1, 4)
    pass1(1, 4)
    pass2(1, 4)
    chain(1, 4)
    pass2(1, 3)
    pass2(1, 2)
    chain(1, 3)
    pass2(1, 1)
    pass2(1, 0)
    chain(1, 2)
    transposed_keys(1)
    grad_q(1)
    dq_give(1).start()
    dq_copy(1).start()
    chain(1, 1)
    chain(1, 0)

    mask_copy.wait_send()
    for hl in range(2):
        for t in range(2):
            qo_wait_send(t, hl)
        dq_give(hl).wait_send()
        dq_copy(hl).wait()
        for kv in range(2):
            for b in range(2):
                own_send(hl, kv, b).wait_send()
            x_send(hl, kv).wait_send()
            for i in range(2):
                for d in range(1, FAR):
                    hop(hl, kv, d, i).wait_send()
                for d in range(1, ND):
                    back(hl, kv, d, i).wait_send()
            g_give(hl, kv).wait_send()
            g_copy(hl, kv).wait()
    for hl in range(2):
        dq_take(hl).wait_recv()
        for kv in range(2):
            g_take(hl, kv).wait_recv()


def per_device(queries, keys, values, segments, loss_mask, grad_out):
    devices = lax.axis_size("cp")
    chips = devices // 2
    dma = pltpu.SemaphoreType.DMA
    anywhere = pl.BlockSpec(memory_space=pl.ANY)
    vmem = pl.BlockSpec(memory_space=pltpu.VMEM)
    return pl.pallas_call(
        functools.partial(kernel, chips),
        out_shape=(
            jax.ShapeDtypeStruct(queries.shape, BF16),
            jax.ShapeDtypeStruct(keys.shape, BF16),
            jax.ShapeDtypeStruct(values.shape, BF16),
        ),
        in_specs=[anywhere, anywhere, anywhere, vmem, vmem, anywhere],
        out_specs=(anywhere, anywhere, anywhere),
        scratch_shapes=[
            pltpu.VMEM((2 * G, BT, HD), BF16),
            pltpu.VMEM((2 * G, BT, HD), BF16),
            pltpu.VMEM((2, 2, ND, BT, HD), BF16),
            pltpu.VMEM((ND, BT, BT), F32),
            pltpu.VMEM((G, ND, BT, BT), F32),
            pltpu.VMEM((G, ND, BT, BT), F32),
            pltpu.VMEM((G, ND * BT, BT), BF16),
            pltpu.VMEM((G, BT, BT), BF16),
            pltpu.VMEM((HD, ND * BT), BF16),
            pltpu.VMEM((ND, G, 1, BT), F32),
            pltpu.VMEM((G, 1, BT), F32),
            pltpu.VMEM((G, 1, BT), F32),
            pltpu.VMEM((2, 2, FAR, BT, HD), BF16),
            pltpu.VMEM((2, 2, FAR, BT, HD), BF16),
            pltpu.VMEM((2, 2, ND, BT, HD), F32),
            pltpu.VMEM((2, 2, BT, HD), BF16),
            pltpu.VMEM((BT, 2 * G * HD), BF16),
            pltpu.VMEM((2, 1, 128), jnp.int32),
            dma((2, 2, ND, 2)), dma((2, 2, 2)), dma((2, 2, FAR - 1, 2)), dma((2, 2)), dma((2, 2)),
            dma((2, 2)), dma((2, 2)), dma((2, 2)), dma, dma,
            dma((2, 2, FAR, 2)), dma((2, 2, FAR, 2)), dma((2,)), dma((2,)), dma((2,)),
            dma((2, 2)), dma((2, 2)), dma((2, 2)),
        ],
        compiler_params=pltpu.CompilerParams(
            collective_id=0, has_side_effects=True, vmem_limit_bytes=58 * 1024 * 1024
        ),
    )(
        queries, keys, values, segments.reshape(devices, 128),
        loss_mask.reshape(1, 128), grad_out,
    )


def solution(mesh):
    tokens = P(("dp", "cp"), None)
    placed = (tokens, tokens, tokens, P("dp"), P(("dp", "cp")), tokens)
    return jax.shard_map(
        per_device, mesh=mesh, in_specs=placed, out_specs=(tokens, tokens, tokens),
        check_vma=False,
    )
```

time: 281 us -> 81.3 us (0.29)
  the two profiles are of different devices: /device:TPU:57 before, /device:TPU:1 now
where the time goes in v1:
time: 81.3 us; the launch traced here: 81 us
  Pallas kernels  76.5 us (94%)
  local copies, waits for them, and re-layouts  3.93 us (5%)
    pallas_call x1, Pallas kernels, per_device(): pl.pallas_call(functools.partial(kernel, chips), out_shape=(jax.ShapeDtyp...  76.5 us
    unnamed x7, local copies, waits for them, and re-layouts  3.93 us

profile of v1, /device:TPU:1, one launch (start us, length us, event | category | flops | bytes accessed | tf_op | source)
XLA Modules:
  0.0 81.0 jit_solution(13711854516334080435)
XLA Ops:
  0.6 76.5 %shard_map.85 = (bf16[128,4096]{1,0:T(8,128)(2,1)}, bf16[128,512]{1,0:T(8,128)(2,1)}, bf16[128,512]{1,0:T(8,128)(2,1)}) custom-call(bf16[128,4096]{1,0:T(8,128)(2,1)} %q_hbm.1, bf16[128,512]{1,0:T(8,128)(2,1)} %k_hbm.1, bf16[128,512]{1,0:T(8,128)(2,1)} %v_hbm.1, s32[64,128]{1,0:T(8,128)} %bitcast.2, s32[1,128]{1,0:T(1,128)} %bitcast.3, bf16[128,4096]{1,0:T(8,128)(2,1)} %do_hbm.1), custom_call_target="tpu_custom_call" | custom-call | tf_op jit(solution)/shard_map/pallas_call | solution.py:394
  77.1 0.0 copy-start.1
  77.1 2.3 %copy.12 = bf16[128,4096]{1,0:T(8,128)(2,1)} copy(bf16[128,4096]{1,0:T(8,128)(2,1)} %get-tuple-element.6) | data formatting | bytes 2097152
  79.4 0.0 copy-done.1
  79.4 0.0 copy-start
  79.4 0.7 copy.13
  80.1 0.3 copy-done
  80.4 0.7 copy.14
Async XLA Ops:
  77.1 2.3 %copy-start.1 = (bf16[128,512]{1,0:T(8,128)(2,1)S(1)}, bf16[128,512]{1,0:T(8,128)(2,1)}, u32[]{:S(2)}) copy-start(bf16[128,512]{1,0:T(8,128)(2,1)} %get-tuple-element.7) | copy-start | bytes 393220
  79.4 1.0 %copy-start = (bf16[128,512]{1,0:T(8,128)(2,1)S(1)}, bf16[128,512]{1,0:T(8,128)(2,1)}, u32[]{:S(2)}) copy-start(bf16[128,512]{1,0:T(8,128)(2,1)} %get-tuple-element.8) | copy-start | bytes 393220

commit v2 on v1

--- a/solution.py
+++ b/solution.py
@@ -14,6 +14,9 @@
 G = 8
 FAR = ND - 1
 NEG = -1e30
+U1 = 4
+U2 = 8
+U3 = 4
 F32 = jnp.float32
 BF16 = jnp.bfloat16
 MESH = pl.DeviceIdType.MESH
@@ -26,12 +29,12 @@
 
 
 def kernel(
-    chips, q_hbm, k_hbm, v_hbm, seg_ref, mask_ref, do_hbm,
+    chips, q_hbm, k_hbm, v_hbm, seg_hbm, mask_hbm, do_hbm,
     dq_out, gk_out, gv_out,
     q_s, o_s, kv_s, bias_s, e_s, dp_s, ds_s, p_s, kt_s, m_s, l_s, dl_s,
-    rbuf, sbuf, gacc, gout, dq_s, mk_s,
+    rbuf, sbuf, gacc, gout, dq_s, mk_s, seg_ref,
     f_recv, f_own, f_relay, f_xsend, f_loc,
-    q_recv, q_send, q_loc, k_recv, k_send,
+    q_recv, q_send, q_loc, k_recv, k_send, s_loc,
     b_recv, b_send, dq_recv, dq_send, dq_loc, g_recv, g_send, g_loc,
 ):
     me = lax.axis_index("cp")
@@ -48,7 +51,6 @@
     barrier = pltpu.get_barrier_semaphore()
     for peer in (partner, after * 2, after * 2 + 1, before * 2, before * 2 + 1):
         pl.semaphore_signal(barrier, inc=1, device_id={"cp": peer}, device_id_type=MESH)
-    pl.semaphore_wait(barrier, 5)
 
     def remote(src, dst, ssem, rsem, cp):
         return pltpu.make_async_remote_copy(
@@ -128,20 +130,19 @@
         rows = held[t].at[hl * G:(hl + 1) * G, theirs, :]
         remote(rows, rows, q_send.at[t, hl], q_recv.at[t, hl], partner).wait_send()
 
-    mask_copy = remote(mask_ref, mk_s.at[core], k_send, k_recv, partner)
-    mask_back = remote(mask_ref, mk_s.at[other], k_send, k_recv, partner)
-
+    mask_copy = remote(mask_hbm, mk_s.at[core], k_send, k_recv, partner)
+    mask_back = remote(mask_hbm, mk_s.at[other], k_send, k_recv, partner)
+
+    seg_copy = pltpu.make_async_copy(seg_hbm, seg_ref, s_loc.at[0])
+    mask_own = pltpu.make_async_copy(mask_hbm, mk_s.at[core], s_loc.at[1])
+    seg_copy.start()
+    mask_own.start()
     for kv in range(2):
-        for b in range(2):
-            own_send(0, kv, b).start()
-    for kv in range(2):
-        x_send(0, kv).start()
         local_kv(0, kv).start()
-    mask_copy.start()
     for t in range(2):
         for i in range(G):
-            qo_send(t, i).start()
             qo_local(t, i).start()
+    seg_copy.wait()
 
     first = 2 * chip - 2 * FAR
 
@@ -158,7 +159,17 @@
         ok = (col == q_seg) & (k_at + offset <= q_at) & (k_at + (first + j) * 128 >= 0)
         bias_s[FAR - j // 2, (j % 2) * 128:(j % 2) * 128 + 128, :] = jnp.where(ok, 0.0, NEG)
 
-    mk_s[pl.ds(core, 1), :, :] = mask_ref[...][None]
+    pl.semaphore_wait(barrier, 5)
+    for kv in range(2):
+        for b in range(2):
+            own_send(0, kv, b).start()
+    for kv in range(2):
+        x_send(0, kv).start()
+    mask_copy.start()
+    for t in range(2):
+        for i in range(G):
+            qo_send(t, i).start()
+    mask_own.wait()
     mask_back.wait_recv()
     mask_col = jnp.concatenate(
         [jnp.broadcast_to(mk_s[i].astype(F32), (128, 128)).T for i in range(2)], axis=0
@@ -183,18 +194,22 @@
 
     c2 = scale * math.log2(math.e)
 
+    def by_eight(x):
+        return x.reshape(BT // 8, 8, BT)
+
     def pass1(hl, d):
         def body(g, carry):
             s = dot(kv_s[hl, 0, d], q_s[hl * G + g], 1, 1)
             dp = dot(kv_s[hl, 1, d], o_s[hl * G + g], 1, 1)
-            x = s * c2 + bias_s[d]
-            peak = jnp.max(x, axis=0, keepdims=True)
+            x = by_eight(s * c2 + bias_s[d])
+            dp = by_eight(dp)
+            peak = jnp.max(x, axis=0)
             if d > 0:
                 old = m_s[d - 1, g]
                 peak = jnp.maximum(old, peak)
-            e = jnp.exp2(x - peak)
-            total = jnp.sum(e, axis=0, keepdims=True)
-            inner = jnp.sum(e * dp, axis=0, keepdims=True)
+            e = jnp.exp2(x - peak[None])
+            total = jnp.sum(e, axis=0)
+            inner = jnp.sum(e * dp, axis=0)
             if d > 0:
                 fade = jnp.exp2(old - peak)
                 total = total + l_s[g] * fade
@@ -202,23 +217,37 @@
             m_s[d, g] = peak
             l_s[g] = total
             dl_s[g] = inner
-            e_s[g, d] = e
-            dp_s[g, d] = dp
+            e_s[g, d] = e.reshape(BT, BT)
+            dp_s[g, d] = dp.reshape(BT, BT)
+            return carry
+        lax.fori_loop(0, G, body, 0, unroll=U1)
+
+    def settle():
+        def body(g, carry):
+            peak = m_s[FAR, g]
+            top = jnp.broadcast_to(jnp.max(peak, axis=0, keepdims=True), (8, BT))
+            fade = jnp.exp2(peak - top)
+            total = jnp.sum(l_s[g] * fade, axis=0, keepdims=True)
+            inner = jnp.sum(dl_s[g] * fade, axis=0, keepdims=True)
+            inv = 1.0 / total
+            dl_s[g] = jnp.broadcast_to(inner * inv, (8, BT))
+            inv = jnp.broadcast_to(inv, (8, BT))
+            for d in range(ND):
+                m_s[d, g] = jnp.exp2(m_s[d, g] - top) * inv
             return carry
         lax.fori_loop(0, G, body, 0)
 
     def pass2(hl, d):
+        span = slice(d * BT, (d + 1) * BT)
         def body(g, carry):
-            inv = 1.0 / l_s[g]
-            f = jnp.exp2(m_s[d, g] - m_s[FAR, g]) * inv
-            delta = dl_s[g] * inv
-            p = e_s[g, d] * f
-            p_s[g] = p.astype(BF16)
-            ds_s[g, d * BT:(d + 1) * BT, :] = (p * (dp_s[g, d] - delta)).astype(BF16)
+            p = by_eight(e_s[g, d]) * m_s[d, g][None]
+            ds = p * (by_eight(dp_s[g, d]) - dl_s[g][None])
+            p_s[g] = p.reshape(BT, BT).astype(BF16)
+            ds_s[hl * G + g, span, :] = ds.reshape(BT, BT).astype(BF16)
             return carry
-        lax.fori_loop(0, G, body, 0)
+        lax.fori_loop(0, G, body, 0, unroll=U2)
         span = slice(hl * G, (hl + 1) * G)
-        ds = jnp.concatenate([ds_s[g, d * BT:(d + 1) * BT, :] for g in range(G)], axis=1)
+        ds = jnp.concatenate([ds_s[hl * G + g, d * BT:(d + 1) * BT, :] for g in range(G)], axis=1)
         gacc[hl, 0, d] = dot(ds, q_s[span].reshape(G * BT, HD), 1, 0)
         p = jnp.concatenate([p_s[g] for g in range(G)], axis=1)
         gacc[hl, 1, d] = dot(p, o_s[span].reshape(G * BT, HD), 1, 0)
@@ -229,10 +258,10 @@
 
     def grad_q(hl):
         def body(g, carry):
-            dqt = dot(kt_s[...], ds_s[g], 1, 0) * scale
+            dqt = dot(kt_s[...], ds_s[hl * G + g], 1, 0) * scale
             dq_s[:, columns(hl * G + g)] = dqt.T.astype(BF16)
             return carry
-        lax.fori_loop(0, G, body, 0)
+        lax.fori_loop(0, G, body, 0, unroll=U3)
 
     def dq_copy(hl):
         return pltpu.make_async_copy(
@@ -320,40 +349,42 @@
         if d == FAR - 1:
             start_second()
         pass1(0, d)
+    settle()
     pass2(0, 4)
     chain(0, 4)
     arrive(1, 0)
     arrive(1, 1)
     pass2(0, 3)
     pass2(0, 2)
+    pass2(0, 1)
+    chain(0, 3)
     arrive(1, 2)
-    chain(0, 3)
-    pass2(0, 1)
     pass2(0, 0)
-    arrive(1, 3)
-    chain(0, 2)
-    transposed_keys(0)
-    grad_q(0)
-    dq_give(0).start()
-    dq_copy(0).start()
     qo_wait(0, 1)
     qo_wait(1, 1)
     mask_grad(1)
     pass1(1, 0)
+    pass1(1, 1)
+    chain(0, 2)
+    arrive(1, 3)
+    pass1(1, 2)
+    pass1(1, 3)
     chain(0, 1)
-    pass1(1, 1)
-    pass1(1, 2)
-    chain(0, 0)
-    pass1(1, 3)
     arrive(1, 4)
     pass1(1, 4)
+    settle()
     pass2(1, 4)
     chain(1, 4)
+    chain(0, 0)
     pass2(1, 3)
     pass2(1, 2)
     chain(1, 3)
     pass2(1, 1)
     pass2(1, 0)
+    transposed_keys(0)
+    grad_q(0)
+    dq_give(0).start()
+    dq_copy(0).start()
     chain(1, 2)
     transposed_keys(1)
     grad_q(1)
@@ -389,17 +420,17 @@
     devices = lax.axis_size("cp")
     chips = devices // 2
     dma = pltpu.SemaphoreType.DMA
-    anywhere = pl.BlockSpec(memory_space=pl.ANY)
+    hbm = pl.BlockSpec(memory_space=pltpu.HBM)
     vmem = pl.BlockSpec(memory_space=pltpu.VMEM)
     return pl.pallas_call(
         functools.partial(kernel, chips),
         out_shape=(
-            jax.ShapeDtypeStruct(queries.shape, BF16),
-            jax.ShapeDtypeStruct(keys.shape, BF16),
-            jax.ShapeDtypeStruct(values.shape, BF16),
+            pltpu.VMEM(queries.shape, BF16),
+            pltpu.VMEM(keys.shape, BF16),
+            pltpu.VMEM(values.shape, BF16),
         ),
-        in_specs=[anywhere, anywhere, anywhere, vmem, vmem, anywhere],
-        out_specs=(anywhere, anywhere, anywhere),
+        in_specs=[hbm] * 6,
+        out_specs=(vmem, vmem, vmem),
         scratch_shapes=[
             pltpu.VMEM((2 * G, BT, HD), BF16),
             pltpu.VMEM((2 * G, BT, HD), BF16),
@@ -407,25 +438,26 @@
             pltpu.VMEM((ND, BT, BT), F32),
             pltpu.VMEM((G, ND, BT, BT), F32),
             pltpu.VMEM((G, ND, BT, BT), F32),
-            pltpu.VMEM((G, ND * BT, BT), BF16),
+            pltpu.VMEM((2 * G, ND * BT, BT), BF16),
             pltpu.VMEM((G, BT, BT), BF16),
             pltpu.VMEM((HD, ND * BT), BF16),
-            pltpu.VMEM((ND, G, 1, BT), F32),
-            pltpu.VMEM((G, 1, BT), F32),
-            pltpu.VMEM((G, 1, BT), F32),
+            pltpu.VMEM((ND, G, 8, BT), F32),
+            pltpu.VMEM((G, 8, BT), F32),
+            pltpu.VMEM((G, 8, BT), F32),
             pltpu.VMEM((2, 2, FAR, BT, HD), BF16),
             pltpu.VMEM((2, 2, FAR, BT, HD), BF16),
             pltpu.VMEM((2, 2, ND, BT, HD), F32),
             pltpu.VMEM((2, 2, BT, HD), BF16),
             pltpu.VMEM((BT, 2 * G * HD), BF16),
             pltpu.VMEM((2, 1, 128), jnp.int32),
+            pltpu.VMEM((devices, 128), jnp.int32),
             dma((2, 2, ND, 2)), dma((2, 2, 2)), dma((2, 2, FAR - 1, 2)), dma((2, 2)), dma((2, 2)),
-            dma((2, 2)), dma((2, 2)), dma((2, 2)), dma, dma,
+            dma((2, 2)), dma((2, 2)), dma((2, 2)), dma, dma, dma((2,)),
             dma((2, 2, FAR, 2)), dma((2, 2, FAR, 2)), dma((2,)), dma((2,)), dma((2,)),
             dma((2, 2)), dma((2, 2)), dma((2, 2)),
         ],
         compiler_params=pltpu.CompilerParams(
-            collective_id=0, has_side_effects=True, vmem_limit_bytes=58 * 1024 * 1024
+            collective_id=0, has_side_effects=True, vmem_limit_bytes=56 * 1024 * 1024
         ),
     )(
         queries, keys, values, segments.reshape(devices, 128),

time: 81.3 us -> 64.3 us (0.79)
  Pallas kernels: 76.5 us -> 61.2 us
  local copies, waits for them, and re-layouts: 3.93 us -> 2.28 us
    pallas_call x1, Pallas kernels: 76.5 us -> 61.2 us  [per_device(): pl.pallas_call(functools.partial(kernel, chips), out_shape=(pltpu.VMEM(qu...]
    unnamed x7 -> x3, local copies, waits for them, and re-layouts: 3.93 us -> 2.28 us
where the time goes in v2:
time: 64.3 us; the launch traced here: 64.1 us
  Pallas kernels  61.2 us (95%)
  local copies, waits for them, and re-layouts  2.28 us (4%)
    pallas_call x1, Pallas kernels, per_device(): pl.pallas_call(functools.partial(kernel, chips), out_shape=(pltpu.VMEM(qu...  61.2 us
    unnamed x3, local copies, waits for them, and re-layouts  2.28 us

profile of v2, /device:TPU:1, one launch (start us, length us, event | category | flops | bytes accessed | tf_op | source)
XLA Modules:
  0.0 64.1 jit_solution(14196500225246050655)
XLA Ops:
  0.6 61.2 %shard_map.85 = (bf16[128,4096]{1,0:T(8,128)(2,1)S(1)}, bf16[128,512]{1,0:T(8,128)(2,1)S(1)}, bf16[128,512]{1,0:T(8,128)(2,1)S(1)}) custom-call(bf16[128,4096]{1,0:T(8,128)(2,1)} %q_hbm.1, bf16[128,512]{1,0:T(8,128)(2,1)} %k_hbm.1, bf16[128,512]{1,0:T(8,128)(2,1)} %v_hbm.1, s32[64,128]{1,0:T(8,128)} %bitcast.2, s32[1,128]{1,0:T(1,128)} %bitcast.3, ...), custom_call_target="tpu_custom_call" | custom-call | tf_op jit(solution)/shard_map/pallas_call | solution.py:425
  61.9 1.0 %copy.12 = bf16[128,4096]{1,0:T(8,128)(2,1)} copy(bf16[128,4096]{1,0:T(8,128)(2,1)S(1)} %get-tuple-element.3) | data formatting | bytes 2097152
  62.8 0.7 %copy.13 = bf16[128,512]{1,0:T(8,128)(2,1)} copy(bf16[128,512]{1,0:T(8,128)(2,1)S(1)} %get-tuple-element.4) | data formatting | bytes 262144
  63.5 0.7 %copy.14 = bf16[128,512]{1,0:T(8,128)(2,1)} copy(bf16[128,512]{1,0:T(8,128)(2,1)S(1)} %get-tuple-element.5) | data formatting | bytes 262144

commit v3 on v2

--- a/solution.py
+++ b/solution.py
@@ -13,6 +13,7 @@
 ND = 5
 G = 8
 FAR = ND - 1
+SIDE = 8
 NEG = -1e30
 U1 = 4
 U2 = 8
@@ -30,12 +31,13 @@
 
 def kernel(
     chips, q_hbm, k_hbm, v_hbm, seg_hbm, mask_hbm, do_hbm,
-    dq_out, gk_out, gv_out,
+    out,
     q_s, o_s, kv_s, bias_s, e_s, dp_s, ds_s, p_s, kt_s, m_s, l_s, dl_s,
-    rbuf, sbuf, gacc, gout, dq_s, mk_s, seg_ref,
+    rbuf, sbuf, gacc, xsend, xback, rlast, mbuf, dq_s, mk_s, seg_ref,
     f_recv, f_own, f_relay, f_xsend, f_loc,
     q_recv, q_send, q_loc, k_recv, k_send, s_loc,
-    b_recv, b_send, dq_recv, dq_send, dq_loc, g_recv, g_send, g_loc,
+    b_recv, b_send, dq_recv, dq_send, dq_loc, g_recv, g_send, l_recv,
+    m_recv, m_own, m_relay,
 ):
     me = lax.axis_index("cp")
     core = me % 2
@@ -45,11 +47,21 @@
     after = (chip + 1) % chips
     before = (chip + chips - 1) % chips
     scale = HD ** -0.5
+
+    def along(who, steps):
+        return who // SIDE * SIDE + (who % SIDE + steps) % SIDE
+
+    mid_to = along(chip, SIDE - 2)
+    mid_from = along(chip, 2)
+    far_to = (mid_from + FAR) % chips
+    far_from = along((chip + chips - FAR) % chips, SIDE - 2)
     mine = pl.ds(pl.multiple_of(core * 128, 128), 128)
     theirs = pl.ds(pl.multiple_of(other * 128, 128), 128)
 
     barrier = pltpu.get_barrier_semaphore()
-    for peer in (partner, after * 2, after * 2 + 1, before * 2, before * 2 + 1):
+    for peer in (
+        partner, after * 2, after * 2 + 1, before * 2, before * 2 + 1,
+    ):
         pl.semaphore_signal(barrier, inc=1, device_id={"cp": peer}, device_id_type=MESH)
 
     def remote(src, dst, ssem, rsem, cp):
@@ -68,6 +80,32 @@
             srcs[kv].at[:, columns(2 * b + hl)], kv_s.at[hl, kv, 1, mine, :],
             f_own.at[hl, kv, b], f_recv.at[hl, kv, 1, core], after * 2 + b,
         )
+
+    def mid_send(kv, b):
+        return remote(
+            srcs[kv].at[:, columns(2 * b)], mbuf.at[kv, mine, :],
+            m_own.at[kv, b], m_recv.at[kv, core], mid_to * 2 + b,
+        )
+
+    def mid_recv(kv, i):
+        return remote(
+            mbuf.at[kv, half(i), :], mbuf.at[kv, half(i), :],
+            m_relay.at[kv, i], m_recv.at[kv, i], mid_to * 2,
+        )
+
+    def mid_hop(kv, i):
+        return remote(
+            mbuf.at[kv, half(i), :], kv_s.at[0, kv, FAR, half(i), :],
+            m_relay.at[kv, i], f_recv.at[0, kv, FAR, i], far_to * 2 + core,
+        )
+
+    def pass_far():
+        for i in range(2):
+            mid_recv(0, i).wait_recv()
+            mid_hop(0, i).start()
+
+    def goes_on(hl, kv, d):
+        return d < FAR
 
     def x_send(hl, kv):
         return remote(
@@ -181,21 +219,26 @@
             return carry
         lax.fori_loop(0, G, body, 0)
 
-    def arrive(hl, d):
-        for kv in range(2):
+    def arrive(hl, d, kvs=(0, 1)):
+        for kv in kvs:
             if d == 0:
                 local_kv(hl, kv).wait()
                 x_recv(hl, kv).wait_recv()
             else:
                 for i in range(2):
                     hop_recv(hl, kv, d, i).wait_recv()
-                    if d < FAR:
+                    if goes_on(hl, kv, d):
                         hop(hl, kv, d, i).start()
 
     c2 = scale * math.log2(math.e)
 
     def by_eight(x):
         return x.reshape(BT // 8, 8, BT)
+
+    def slot(hl, d):
+        if hl == 0:
+            return d
+        return ND if d == FAR else FAR - d
 
     def pass1(hl, d):
         def body(g, carry):
@@ -205,52 +248,82 @@
             dp = by_eight(dp)
             peak = jnp.max(x, axis=0)
             if d > 0:
-                old = m_s[d - 1, g]
+                old = m_s[hl, d - 1, g]
                 peak = jnp.maximum(old, peak)
             e = jnp.exp2(x - peak[None])
             total = jnp.sum(e, axis=0)
             inner = jnp.sum(e * dp, axis=0)
             if d > 0:
                 fade = jnp.exp2(old - peak)
-                total = total + l_s[g] * fade
-                inner = inner + dl_s[g] * fade
-            m_s[d, g] = peak
-            l_s[g] = total
-            dl_s[g] = inner
-            e_s[g, d] = e.reshape(BT, BT)
-            dp_s[g, d] = dp.reshape(BT, BT)
+                total = total + l_s[hl, g] * fade
+                inner = inner + dl_s[hl, g] * fade
+            m_s[hl, d, g] = peak
+            l_s[hl, g] = total
+            dl_s[hl, g] = inner
+            e_s[g, slot(hl, d)] = e.reshape(BT, BT)
+            dp_s[g, slot(hl, d)] = dp.reshape(BT, BT)
             return carry
         lax.fori_loop(0, G, body, 0, unroll=U1)
 
-    def settle():
+    def scores_only(hl):
         def body(g, carry):
-            peak = m_s[FAR, g]
+            s = dot(kv_s[hl, 0, FAR], q_s[hl * G + g], 1, 1)
+            x = by_eight(s * c2 + bias_s[FAR])
+            old = m_s[hl, FAR - 1, g]
+            peak = jnp.maximum(old, jnp.max(x, axis=0))
+            e = jnp.exp2(x - peak[None])
+            fade = jnp.exp2(old - peak)
+            l_s[hl, g] = jnp.sum(e, axis=0) + l_s[hl, g] * fade
+            dl_s[hl, g] = dl_s[hl, g] * fade
+            m_s[hl, FAR, g] = peak
+            e_s[g, slot(hl, FAR)] = e.reshape(BT, BT)
+            return carry
+        lax.fori_loop(0, G, body, 0, unroll=U1)
+
+    def dprobs_only(hl):
+        def body(g, carry):
+            dp = by_eight(dot(kv_s[hl, 1, FAR], o_s[hl * G + g], 1, 1))
+            inner = jnp.sum(by_eight(e_s[g, slot(hl, FAR)]) * dp, axis=0) + dl_s[hl, g]
+            delta = jnp.sum(inner * m_s[hl, FAR, g], axis=0, keepdims=True)
+            dl_s[hl, g] = jnp.broadcast_to(delta, (8, BT))
+            dp_s[g, slot(hl, FAR)] = dp.reshape(BT, BT)
+            return carry
+        lax.fori_loop(0, G, body, 0, unroll=U1)
+
+    def settle(hl, delta=True):
+        def body(g, carry):
+            peak = m_s[hl, FAR, g]
             top = jnp.broadcast_to(jnp.max(peak, axis=0, keepdims=True), (8, BT))
             fade = jnp.exp2(peak - top)
-            total = jnp.sum(l_s[g] * fade, axis=0, keepdims=True)
-            inner = jnp.sum(dl_s[g] * fade, axis=0, keepdims=True)
+            total = jnp.sum(l_s[hl, g] * fade, axis=0, keepdims=True)
             inv = 1.0 / total
-            dl_s[g] = jnp.broadcast_to(inner * inv, (8, BT))
+            if delta:
+                inner = jnp.sum(dl_s[hl, g] * fade, axis=0, keepdims=True)
+                dl_s[hl, g] = jnp.broadcast_to(inner * inv, (8, BT))
             inv = jnp.broadcast_to(inv, (8, BT))
             for d in range(ND):
-                m_s[d, g] = jnp.exp2(m_s[d, g] - top) * inv
+                m_s[hl, d, g] = jnp.exp2(m_s[hl, d, g] - top) * inv
             return carry
         lax.fori_loop(0, G, body, 0)
 
-    def pass2(hl, d):
-        span = slice(d * BT, (d + 1) * BT)
+    def pass2(hl, d, kvs=(0, 1)):
+        keys = slice(d * BT, (d + 1) * BT)
         def body(g, carry):
-            p = by_eight(e_s[g, d]) * m_s[d, g][None]
-            ds = p * (by_eight(dp_s[g, d]) - dl_s[g][None])
-            p_s[g] = p.reshape(BT, BT).astype(BF16)
-            ds_s[hl * G + g, span, :] = ds.reshape(BT, BT).astype(BF16)
+            p = by_eight(e_s[g, slot(hl, d)]) * m_s[hl, d, g][None]
+            if 1 in kvs:
+                p_s[g] = p.reshape(BT, BT).astype(BF16)
+            if 0 in kvs:
+                ds = p * (by_eight(dp_s[g, slot(hl, d)]) - dl_s[hl, g][None])
+                ds_s[hl * G + g, keys, :] = ds.reshape(BT, BT).astype(BF16)
             return carry
         lax.fori_loop(0, G, body, 0, unroll=U2)
         span = slice(hl * G, (hl + 1) * G)
-        ds = jnp.concatenate([ds_s[hl * G + g, d * BT:(d + 1) * BT, :] for g in range(G)], axis=1)
-        gacc[hl, 0, d] = dot(ds, q_s[span].reshape(G * BT, HD), 1, 0)
-        p = jnp.concatenate([p_s[g] for g in range(G)], axis=1)
-        gacc[hl, 1, d] = dot(p, o_s[span].reshape(G * BT, HD), 1, 0)
+        if 0 in kvs:
+            ds = jnp.concatenate([ds_s[hl * G + g, keys, :] for g in range(G)], axis=1)
+            gacc[hl, 0, d] = dot(ds, q_s[span].reshape(G * BT, HD), 1, 0)
+        if 1 in kvs:
+            p = jnp.concatenate([p_s[g] for g in range(G)], axis=1)
+            gacc[hl, 1, d] = dot(p, o_s[span].reshape(G * BT, HD), 1, 0)
 
     def transposed_keys(hl):
         for d in range(ND):
@@ -260,26 +333,21 @@
         def body(g, carry):
             dqt = dot(kt_s[...], ds_s[hl * G + g], 1, 0) * scale
             dq_s[:, columns(hl * G + g)] = dqt.T.astype(BF16)
+            out[:, columns(core * 16 + hl * G + g)] = dq_s[mine, columns(hl * G + g)]
             return carry
         lax.fori_loop(0, G, body, 0, unroll=U3)
 
-    def dq_copy(hl):
-        return pltpu.make_async_copy(
-            dq_s.at[mine, columns(hl * G, G)],
-            dq_out.at[:, columns(core * 16 + hl * G, G)], dq_loc.at[hl],
-        )
-
     def dq_give(hl):
         return remote(
             dq_s.at[theirs, columns(hl * G, G)],
-            dq_out.at[:, columns(core * 16 + hl * G, G)],
+            out.at[:, columns(core * 16 + hl * G, G)],
             dq_send.at[hl], dq_recv.at[hl], partner,
         )
 
     def dq_take(hl):
         return remote(
             dq_s.at[theirs, columns(hl * G, G)],
-            dq_out.at[:, columns(other * 16 + hl * G, G)],
+            out.at[:, columns(other * 16 + hl * G, G)],
             dq_send.at[hl], dq_recv.at[hl], partner,
         )
 
@@ -290,49 +358,57 @@
             before * 2 + core,
         )
 
-    outs = (gk_out, gv_out)
-
-    def g_copy(hl, kv):
-        return pltpu.make_async_copy(
-            gout.at[hl, kv, mine, :], outs[kv].at[:, columns(2 * core + hl)],
-            g_loc.at[hl, kv],
+    def last(hl, kv, i):
+        return remote(
+            sbuf.at[hl, kv, 0, half(i), :], rlast.at[hl, kv, core],
+            b_send.at[hl, kv, 0, i], l_recv.at[hl, kv, core], before * 2 + i,
+        )
+
+    def last_recv(hl, kv, i):
+        return remote(
+            sbuf.at[hl, kv, 0, half(i), :], rlast.at[hl, kv, i],
+            b_send.at[hl, kv, 0, i], l_recv.at[hl, kv, i], before * 2 + i,
         )
 
     def g_give(hl, kv):
         return remote(
-            gout.at[hl, kv, theirs, :], outs[kv].at[:, columns(2 * core + hl)],
+            xsend.at[hl, kv], xback.at[hl, kv],
             g_send.at[hl, kv], g_recv.at[hl, kv], partner,
         )
 
-    def g_take(hl, kv):
-        return remote(
-            gout.at[hl, kv, theirs, :], outs[kv].at[:, columns(2 * other + hl)],
-            g_send.at[hl, kv], g_recv.at[hl, kv], partner,
-        )
-
-    def chain(hl, d):
+    def own_block(hl):
         for kv in range(2):
+            xsend[hl, kv] = gacc[hl, kv, 0, theirs, :].astype(BF16)
+            g_give(hl, kv).start()
+
+    def link(hl, d, kv, i):
+        rows = slice(i * 128, i * 128 + 128)
+        part = gacc[hl, kv, d, rows, :]
+        if d < FAR:
+            back(hl, kv, d + 1, i).wait_recv()
+            part = part + rbuf[hl, kv, d, rows, :].astype(F32)
+        sbuf[hl, kv, d - 1, rows, :] = part.astype(BF16)
+        if d > 1:
+            back(hl, kv, d, i).start()
+        else:
+            last(hl, kv, i).start()
+
+    def chain(hl, d, kvs=(1, 0)):
+        for kv in kvs:
             for i in range(2):
-                rows = slice(i * 128, i * 128 + 128)
-                part = gacc[hl, kv, d, rows, :]
-                if d < FAR:
-                    back(hl, kv, d + 1, i).wait_recv()
-                    part = part + rbuf[hl, kv, d, rows, :].astype(F32)
-                if d > 0:
-                    sbuf[hl, kv, d - 1, rows, :] = part.astype(BF16)
-                    back(hl, kv, d, i).start()
-                else:
-                    if kv == 0:
-                        part = part * scale
-                    gout[hl, kv, rows, :] = part.astype(BF16)
-            if d == 0:
-                g_give(hl, kv).start()
-                g_copy(hl, kv).start()
+                link(hl, d, kv, i)
+
+    def finish(hl, kv):
+        factor = scale if kv == 0 else 1.0
+        g_give(hl, kv).wait_recv()
+        for i in range(2):
+            last_recv(hl, kv, i).wait_recv()
+        part = gacc[hl, kv, 0, mine, :] + rlast[hl, kv, core].astype(F32)
+        out[:, columns(32 + 4 * kv + 2 * core + hl)] = (part * factor).astype(BF16)
+        part = xback[hl, kv].astype(F32) + rlast[hl, kv, other].astype(F32)
+        out[:, columns(32 + 4 * kv + 2 * other + hl)] = (part * factor).astype(BF16)
 
     def start_second():
-        for kv in range(2):
-            for b in range(2):
-                own_send(1, kv, b).start()
         for kv in range(2):
             x_send(1, kv).start()
             local_kv(1, kv).start()
@@ -344,76 +420,92 @@
     qo_wait(0, 0)
     qo_wait(1, 0)
     mask_grad(0)
-    for d in range(ND):
-        arrive(0, d)
-        if d == FAR - 1:
-            start_second()
-        pass1(0, d)
-    settle()
+    arrive(0, 0)
+    pass1(0, 0)
+    arrive(0, 1)
+    pass1(0, 1)
+    arrive(0, 2)
+    pass1(0, 2)
+    arrive(0, 3)
+    own_send(1, 0, 0).start()
+    own_send(1, 0, 1).start()
+    own_send(1, 1, 0).start()
+    own_send(1, 1, 1).start()
+    start_second()
+    pass1(0, 3)
+    arrive(0, 4)
+    pass1(0, 4)
+    arrive(1, 1)
+    settle(0)
     pass2(0, 4)
     chain(0, 4)
-    arrive(1, 0)
-    arrive(1, 1)
     pass2(0, 3)
+    arrive(1, 2)
     pass2(0, 2)
     pass2(0, 1)
     chain(0, 3)
-    arrive(1, 2)
-    pass2(0, 0)
+    arrive(1, 0)
+    arrive(1, 3)
     qo_wait(0, 1)
     qo_wait(1, 1)
     mask_grad(1)
     pass1(1, 0)
     pass1(1, 1)
     chain(0, 2)
-    arrive(1, 3)
     pass1(1, 2)
     pass1(1, 3)
-    chain(0, 1)
-    arrive(1, 4)
-    pass1(1, 4)
-    settle()
-    pass2(1, 4)
-    chain(1, 4)
-    chain(0, 0)
+    arrive(1, 4, (0,))
+    scores_only(1)
+    settle(1, False)
+    pass2(1, 4, (1,))
+    chain(1, 4, (1,))
+    arrive(1, 4, (1,))
+    link(0, 1, 1, 0)
+    dprobs_only(1)
+    pass2(1, 4, (0,))
+    chain(1, 4, (0,))
+    link(0, 1, 1, 1)
     pass2(1, 3)
+    pass2(0, 0)
     pass2(1, 2)
     chain(1, 3)
-    pass2(1, 1)
-    pass2(1, 0)
+    link(0, 1, 0, 0)
+    link(0, 1, 0, 1)
+    own_block(0)
     transposed_keys(0)
     grad_q(0)
     dq_give(0).start()
-    dq_copy(0).start()
+    pass2(1, 1)
     chain(1, 2)
+    pass2(1, 0)
+    own_block(1)
     transposed_keys(1)
     grad_q(1)
     dq_give(1).start()
-    dq_copy(1).start()
     chain(1, 1)
-    chain(1, 0)
-
+    finish(0, 0)
+    finish(0, 1)
     mask_copy.wait_send()
     for hl in range(2):
         for t in range(2):
             qo_wait_send(t, hl)
         dq_give(hl).wait_send()
-        dq_copy(hl).wait()
         for kv in range(2):
             for b in range(2):
                 own_send(hl, kv, b).wait_send()
             x_send(hl, kv).wait_send()
             for i in range(2):
                 for d in range(1, FAR):
-                    hop(hl, kv, d, i).wait_send()
-                for d in range(1, ND):
+                    if goes_on(hl, kv, d):
+                        hop(hl, kv, d, i).wait_send()
+                for d in range(2, ND):
                     back(hl, kv, d, i).wait_send()
+                last(hl, kv, i).wait_send()
             g_give(hl, kv).wait_send()
-            g_copy(hl, kv).wait()
     for hl in range(2):
         dq_take(hl).wait_recv()
-        for kv in range(2):
-            g_take(hl, kv).wait_recv()
+    for kv in (1, 0):
+        finish(1, kv)
 
 
 def per_device(queries, keys, values, segments, loss_mask, grad_out):
@@ -422,39 +514,41 @@
     dma = pltpu.SemaphoreType.DMA
     hbm = pl.BlockSpec(memory_space=pltpu.HBM)
     vmem = pl.BlockSpec(memory_space=pltpu.VMEM)
-    return pl.pallas_call(
+    (joined,) = pl.pallas_call(
         functools.partial(kernel, chips),
         out_shape=(
-            pltpu.VMEM(queries.shape, BF16),
-            pltpu.VMEM(keys.shape, BF16),
-            pltpu.VMEM(values.shape, BF16),
+            pltpu.VMEM((queries.shape[0], queries.shape[1] + 2 * keys.shape[1]), BF16),
         ),
         in_specs=[hbm] * 6,
-        out_specs=(vmem, vmem, vmem),
+        out_specs=(vmem,),
         scratch_shapes=[
             pltpu.VMEM((2 * G, BT, HD), BF16),
             pltpu.VMEM((2 * G, BT, HD), BF16),
             pltpu.VMEM((2, 2, ND, BT, HD), BF16),
             pltpu.VMEM((ND, BT, BT), F32),
-            pltpu.VMEM((G, ND, BT, BT), F32),
-            pltpu.VMEM((G, ND, BT, BT), F32),
+            pltpu.VMEM((G, ND + 1, BT, BT), F32),
+            pltpu.VMEM((G, ND + 1, BT, BT), F32),
             pltpu.VMEM((2 * G, ND * BT, BT), BF16),
             pltpu.VMEM((G, BT, BT), BF16),
             pltpu.VMEM((HD, ND * BT), BF16),
-            pltpu.VMEM((ND, G, 8, BT), F32),
-            pltpu.VMEM((G, 8, BT), F32),
-            pltpu.VMEM((G, 8, BT), F32),
+            pltpu.VMEM((2, ND, G, 8, BT), F32),
+            pltpu.VMEM((2, G, 8, BT), F32),
+            pltpu.VMEM((2, G, 8, BT), F32),
             pltpu.VMEM((2, 2, FAR, BT, HD), BF16),
             pltpu.VMEM((2, 2, FAR, BT, HD), BF16),
             pltpu.VMEM((2, 2, ND, BT, HD), F32),
-            pltpu.VMEM((2, 2, BT, HD), BF16),
+            pltpu.VMEM((2, 2, 128, HD), BF16),
+            pltpu.VMEM((2, 2, 128, HD), BF16),
+            pltpu.VMEM((2, 2, 2, 128, HD), BF16),
+            pltpu.VMEM((1, BT, HD), BF16),
             pltpu.VMEM((BT, 2 * G * HD), BF16),
             pltpu.VMEM((2, 1, 128), jnp.int32),
             pltpu.VMEM((devices, 128), jnp.int32),
             dma((2, 2, ND, 2)), dma((2, 2, 2)), dma((2, 2, FAR - 1, 2)), dma((2, 2)), dma((2, 2)),
             dma((2, 2)), dma((2, 2)), dma((2, 2)), dma, dma, dma((2,)),
             dma((2, 2, FAR, 2)), dma((2, 2, FAR, 2)), dma((2,)), dma((2,)), dma((2,)),
-            dma((2, 2)), dma((2, 2)), dma((2, 2)),
+            dma((2, 2)), dma((2, 2)), dma((2, 2, 2)),
+            dma((1, 2)), dma((1, 2)), dma((1, 2)),
         ],
         compiler_params=pltpu.CompilerParams(
             collective_id=0, has_side_effects=True, vmem_limit_bytes=56 * 1024 * 1024
@@ -463,6 +557,10 @@
         queries, keys, values, segments.reshape(devices, 128),
         loss_mask.reshape(1, 128), grad_out,
     )
+    wide, narrow = queries.shape[1], keys.shape[1]
+    return (
+        joined[:, :wide], joined[:, wide:wide + narrow], joined[:, wide + narrow:],
+    )
 
 
 def solution(mesh):

time: 64.3 us -> 62.4 us (0.970)
  Pallas kernels: 61.2 us -> 59.8 us
    unnamed x3 -> x0, local copies, waits for them, and re-layouts: 2.28 us -> none
    slice x0 -> x2, local copies, waits for them, and re-layouts: none -> 1.76 us  [the longest x1 1.04 us: per_device(): joined[:, :wide]]
    pallas_call x1, Pallas kernels: 61.2 us -> 59.8 us  [per_device(): pl.pallas_call(functools.partial(kernel, chips), out_shape=(pltpu.VMEM((q...]
where the time goes in v3:
time: 62.4 us; the launch traced here: 62.2 us
  Pallas kernels  59.8 us (96%)
  local copies, waits for them, and re-layouts  1.76 us (3%)
  between operations  0.64 us (1%)
    pallas_call x1, Pallas kernels, per_device(): pl.pallas_call(functools.partial(kernel, chips), out_shape=(pltpu.VMEM((q...  59.8 us

profile of v3, /device:TPU:1, one launch (start us, length us, event | category | flops | bytes accessed | tf_op | source)
XLA Modules:
  0.0 62.2 jit_solution(18043030800469071308)
XLA Ops:
  0.6 59.8 %shard_map.85 = bf16[128,5120]{1,0:T(8,128)(2,1)S(1)} custom-call(bf16[128,4096]{1,0:T(8,128)(2,1)} %q_hbm.1, bf16[128,512]{1,0:T(8,128)(2,1)} %k_hbm.1, bf16[128,512]{1,0:T(8,128)(2,1)} %v_hbm.1, s32[64,128]{1,0:T(8,128)} %bitcast.2, s32[1,128]{1,0:T(1,128)} %bitcast.3, bf16[128,4096]{1,0:T(8,128)(2,1)} %do_hbm.1), custom_call_target="tpu_custom_call" | custom-call | tf_op jit(solution)/shard_map/pallas_call | solution.py:517
  60.5 0.7 %fusion = (bf16[128,512]{1,0:T(8,128)(2,1)}, bf16[128,512]{1,0:T(8,128)(2,1)}) fusion(bf16[128,5120]{1,0:T(8,128)(2,1)S(1)} %shard_map.85), kind=kLoop, calls=%fused_computation | loop fusion | bytes 524288 | tf_op jit(solution)/shard_map/slice | solution.py:562
  61.2 1.0 %slice.9 = bf16[128,4096]{1,0:T(8,128)(2,1)} slice(bf16[128,5120]{1,0:T(8,128)(2,1)S(1)} %shard_map.85), slice={[0:128], [0:4096]} | slice | bytes 2097152 | tf_op jit(solution)/shard_map/slice | solution.py:562
